TPU v7x, 256 devices: a whole 4x4x8 slice. The times are simulated.
256 devices in a mesh: ax: 64 (over x, y, z_lo, core), az: 4 (over z_hi).
Axes of the slice: x: 4, y: 4, z: 8 (z_hi: 4, z_lo: 2; z = z_hi * 2 + z_lo), core: 2. Of those that a mesh axis runs over, the one named last changes fastest.
Arguments:
- phase_field: float32 [1024, 256, 512], P('ax', None, 'az'), may hold values from -6 to 6
- section_cotangent: float32 [1024, 256, 512], P('ax', None, 'az'), may hold values from -6 to 6
Outputs:
- phase_gradient: float32 [1024, 256, 512], P('ax', None, 'az')
All inputs are finite; a program needn't handle non-finite values.
Results may differ from a plain program's by a relative error of at most 0.00012.
Values sent between devices are 32-bit elements; how exact they have to be, the bound alone decides.
No kernel may reach another device: no remote copies, remote signals or barrier semaphores. Data moves between devices by JAX's collectives and lax.ppermute only.
A program may use at most 64 MiB of HBM per device.

v0:
```python
import math

import jax
import jax.numpy as jnp
from jax import lax
from jax.sharding import PartitionSpec as P

NX = 1024
NY = 512
NR = 256


def radial_table_at(count, points):
    modes = jnp.arange(count, dtype=jnp.float32)[:, None]
    weight = jnp.where(modes == 0, math.sqrt(1.0 / count), math.sqrt(2.0 / count))
    return weight * jnp.cos(math.pi * modes * (points[None, :] + 0.5) / count)


def fourier_table(count):
    half = count // 2
    modes = lax.iota(jnp.int32, count)[:, None]
    points = lax.iota(jnp.int32, count)[None, :]
    wave = jnp.where(modes <= half, modes, modes - half)
    turns = wave * points % count
    angle = 2.0 * math.pi / count * turns.astype(jnp.float32)
    scale = jnp.where(
        (modes == 0) | (modes == half), math.sqrt(1.0 / count), math.sqrt(2.0 / count)
    )
    return scale * jnp.where(modes <= half, jnp.cos(angle), jnp.sin(angle))


def per_device(phase_field, section_cotangent):
    highest = lax.Precision.HIGHEST
    radial = radial_table_at(NR, jnp.arange(NR, dtype=jnp.float32))
    axial = fourier_table(NX)
    azimuth = fourier_table(NY)
    state_radial = jnp.einsum("xmy,mj->xjy", phase_field, radial, precision=highest)
    adjoint_radial = jnp.einsum("xmy,mj->xjy", section_cotangent, radial, precision=highest)
    fields = (
        lax.all_to_all(state_radial, "az", split_axis=1, concat_axis=2, tiled=True),
        lax.all_to_all(adjoint_radial, "az", split_axis=1, concat_axis=2, tiled=True),
    )
    state_lines, adjoint_lines = tuple(
        (jnp.einsum("xrm,my->xry", field, azimuth, precision=highest) for field in fields)
    )
    fields = (
        lax.all_to_all(state_lines, "ax", split_axis=1, concat_axis=0, tiled=True),
        lax.all_to_all(adjoint_lines, "ax", split_axis=1, concat_axis=0, tiled=True),
    )
    state_grid, adjoint_grid = tuple(
        (jnp.einsum("mry,mx->xry", field, axial, precision=highest) for field in fields)
    )
    weighted = (3.0 * state_grid * state_grid - 1.0) * adjoint_grid
    axial_coeffs = jnp.einsum("xry,mx->mry", weighted, axial, precision=highest)
    both_coeffs = jnp.einsum("xry,my->xrm", axial_coeffs, azimuth, precision=highest)
    mixed = lax.all_to_all(both_coeffs, "ax", split_axis=0, concat_axis=1, tiled=True)
    return jnp.einsum(
        "xjy,mj->xmy",
        lax.all_to_all(mixed, "az", split_axis=2, concat_axis=1, tiled=True),
        radial,
        precision=highest,
    )


def solution(mesh):
    in_specs = (P("ax", None, "az"), P("ax", None, "az"))
    out_specs = P("ax", None, "az")
    return jax.shard_map(
        per_device, mesh=mesh, in_specs=in_specs, out_specs=out_specs, check_vma=False
    )
```

profile of v0, /device:TPU:1, one launch (start us, length us, event | category | flops | bytes accessed | tf_op | source)
XLA Modules:
  0.0 379.4 jit_solution(3050518954088438978)
XLA Ops:
  0.0 0.0 copy-start
  0.0 1.6 copy-done
  1.6 2.9 convolution_bitcast_fusion.3
  4.5 2.6 copy.27
  7.0 9.0 %all-to-all-start = ((f32[16,256,128]{2,0,1:T(8,128)}), f32[16,256,128]{2,0,1:T(8,128)S(1)}, u32[]{:S(2)}, u32[]{:S(2)}) async-start(f32[16,256,128]{2,0,1:T(8,128)} %copy.27), calls=%async_computation | async-start | bytes 4194304 | tf_op jit(solution)/shard_map/all_to_all | solution.py:40
  16.0 4.4 %convolution_bitcast_fusion.2 = f32[16,256,128]{2,1,0:T(8,128)S(1)} fusion(f32[16,256,128]{2,1,0:T(8,128)} %param.3, f32[256]{0:T(256)S(1)} %get-tuple-element.6, f32[256]{0:T(256)S(1)} %iota_multiply_fusion, f32[256]{0:T(256)S(1)} %get-tuple-element.5), kind=kOutput, calls=%fused_computation.24 | convolution fusion | flops 1610809344 | bytes 4197376 | tf_op jit(solution)/shard_map/xmy,mj->xjy/dot_general | solution.py:38
  20.5 2.5 copy.31
  23.0 34.9 %all-to-all-done = f32[16,256,128]{2,0,1:T(8,128)S(1)} async-done(((f32[16,256,128]{2,0,1:T(8,128)}), f32[16,256,128]{2,0,1:T(8,128)S(1)}, u32[]{:S(2)}, u32[]{:S(2)}) %all-to-all-start) | async-done | bytes 2097184 | tf_op jit(solution)/shard_map/all_to_all | solution.py:40
  57.9 0.0 copy-start.2
  57.9 1.3 copy-done.2
  59.2 10.2 %all-to-all-start.2 = ((f32[16,256,128]{2,0,1:T(8,128)}), f32[16,256,128]{2,0,1:T(8,128)S(1)}, u32[]{:S(2)}, u32[]{:S(2)}) async-start(f32[16,256,128]{2,0,1:T(8,128)} %copy.31), calls=%async_computation.2 | async-start | bytes 4194304 | tf_op jit(solution)/shard_map/all_to_all | solution.py:41
  69.5 4.3 %copy.52 = f32[16,4,64,128]{3,1,2,0:T(4,128)} copy(f32[16,4,64,128]{3,0,2,1:T(8,128)} %bitcast.64) | data formatting | bytes 4194304 | tf_op jit(solution)/shard_map/all_to_all | solution.py:40
  73.8 3.1 all_to_all.77
  76.9 11.6 %fusion.12 = f32[16,64,512]{2,0,1:T(8,128)} fusion(f32[16,64,512]{2,1,0:T(8,128)} %all_to_all.77, s32[512]{0:T(512)S(1)} %add_select_fusion.3, f32[512]{0:T(512)S(1)} %fusion.44, pred[512]{0:T(512)(128)(4,1)S(1)} %iota_compare_fusion.5), kind=kOutput, calls=%fused_computation.16 | convolution fusion | flops 3225419776 | bytes 4198912 | tf_op jit(solution)/shard_map/xrm,my->xry/dot_general | solution.py:44
  88.4 11.6 %all-to-all-done.2 = f32[16,256,128]{2,0,1:T(8,128)S(1)} async-done(((f32[16,256,128]{2,0,1:T(8,128)}), f32[16,256,128]{2,0,1:T(8,128)S(1)}, u32[]{:S(2)}, u32[]{:S(2)}) %all-to-all-start.2) | async-done | bytes 2097184 | tf_op jit(solution)/shard_map/all_to_all | solution.py:41
  100.0 30.0 %all-to-all-start.1 = ((f32[16,64,512]{2,0,1:T(8,128)}), f32[16,64,512]{2,0,1:T(8,128)}, u32[]{:S(2)}, u32[]{:S(2)}) async-start(f32[16,64,512]{2,0,1:T(8,128)} %fusion.12), calls=%async_computation.1 | async-start | bytes 4194304 | tf_op jit(solution)/shard_map/all_to_all | solution.py:47
  130.0 2.7 copy.51
  132.7 2.1 all_to_all.84
  134.8 10.0 %fusion.10 = f32[16,64,512]{2,0,1:T(8,128)} fusion(f32[16,64,512]{2,1,0:T(8,128)S(1)} %all_to_all.84, s32[512]{0:T(512)S(1)} %add_select_fusion.3, f32[512]{0:T(512)S(1)} %fusion.44, pred[512]{0:T(512)(128)(4,1)S(1)} %iota_compare_fusion.5), kind=kOutput, calls=%fused_computation.14 | convolution fusion | flops 3225419776 | bytes 4198912 | tf_op jit(solution)/shard_map/xrm,my->xry/dot_general | solution.py:44
  144.8 14.4 %all-to-all-done.1 = f32[16,64,512]{2,0,1:T(8,128)} async-done(((f32[16,64,512]{2,0,1:T(8,128)}), f32[16,64,512]{2,0,1:T(8,128)}, u32[]{:S(2)}, u32[]{:S(2)}) %all-to-all-start.1) | async-done | bytes 2097184 | tf_op jit(solution)/shard_map/all_to_all | solution.py:47
  159.2 5.4 %all-to-all-start.3 = ((f32[16,64,512]{2,0,1:T(8,128)}), f32[16,64,512]{2,0,1:T(8,128)}, u32[]{:S(2)}, u32[]{:S(2)}) async-start(f32[16,64,512]{2,0,1:T(8,128)} %fusion.10), calls=%async_computation.3 | async-start | bytes 4194304 | tf_op jit(solution)/shard_map/all_to_all | solution.py:48
  164.6 25.7 %fusion.15 = f32[1024,512]{1,0:T(8,128)S(1)} fusion(f32[1024,512]{1,0:T(8,128)} %bitcast.8, s32[1024]{0:T(1024)S(1)} %add_select_fusion.2, f32[1024]{0:T(1024)S(1)} %fusion.42, pred[1024]{0:T(1024)(128)(4,1)S(1)} %iota_compare_fusion.2), kind=kOutput, calls=%fused_computation.21 | convolution fusion | flops 6459228160 | bytes 4203520 | tf_op jit(solution)/shard_map/mry,mx->xry/dot_general | solution.py:51
  190.3 3.7 all-to-all-done.3
  194.0 26.0 %fusion.14 = f32[1024,512]{1,0:T(8,128)S(1)} fusion(f32[1024,512]{1,0:T(8,128)} %bitcast.15, s32[1024]{0:T(1024)S(1)} %add_select_fusion.2, f32[1024]{0:T(1024)S(1)} %fusion.42, pred[1024]{0:T(1024)(128)(4,1)S(1)} %iota_compare_fusion.2), kind=kOutput, calls=%fused_computation.20 | convolution fusion | flops 6459228160 | bytes 4203520 | tf_op jit(solution)/shard_map/mry,mx->xry/dot_general | solution.py:51
  220.1 0.5 fusion.84
  220.6 24.5 %fusion.8 = f32[1024,512]{1,0:T(8,128)S(1)} fusion(s32[1024]{0:T(1024)S(1)} %add_select_fusion.2, f32[1024]{0:T(1024)S(1)} %fusion.42, pred[1024]{0:T(1024)(128)(4,1)S(1)} %iota_compare_fusion.2, f32[1024,512]{1,0:T(8,128)S(1)} %fusion.84), kind=kOutput, calls=%fused_computation.13 | convolution fusion | flops 6459228160 | bytes 4203520 | tf_op jit(solution)/shard_map/xry,mx->mry/dot_general | solution.py:54
  245.0 9.4 %convolution_bitcast_fusion = f32[1024,1,512]{2,0,1:T(8,128)S(1)} fusion(f32[1024,512]{1,0:T(8,128)S(1)} %fusion.8, s32[512]{0:T(512)S(1)} %add_select_fusion.3, f32[512]{0:T(512)S(1)} %fusion.44, pred[512]{0:T(512)(128)(4,1)S(1)} %iota_compare_fusion.5), kind=kOutput, calls=%fused_computation.22 | convolution fusion | flops 3225419776 | bytes 4198912 | tf_op jit(solution)/shard_map/xry,my->xrm/dot_general | solution.py:55
  254.4 2.2 copy.34
  256.6 34.5 %all_to_all.102 = f32[1024,1,512]{2,1,0:T(1,128)S(1)} all-to-all(f32[1024,1,512]{2,1,0:T(1,128)S(1)} %copy.34), channel_id=1, replica_groups=mesh['ax'=64,'az'=4] {'ax'}, dimensions={0} | all-to-all | bytes 4194304 | tf_op jit(solution)/shard_map/all_to_all | solution.py:56
  291.1 5.2 %copy.35 = f32[64,16,1,512]{0,1,3,2:T(8,128)} copy(f32[64,16,1,512]{3,2,1,0:T(1,128)S(1)} %bitcast.62) | data formatting | bytes 4194304 | tf_op jit(solution)/shard_map/all_to_all | solution.py:56
  296.3 4.4 %bitcast_bitcast_fusion = f32[512,16,64]{2,1,0:T(8,128)} fusion(f32[64,16,1,512]{0,1,3,2:T(8,128)} %copy.35), kind=kLoop, calls=%fused_computation.100 | loop fusion | bytes 4194304
  300.7 4.5 %reshape.97 = f32[4,1,131072]{2,1,0:T(1,128)S(1)} reshape(f32[512,16,64]{2,1,0:T(8,128)} %bitcast_bitcast_fusion) | data formatting | bytes 4194304
  305.2 51.9 %all_to_all.103 = f32[4,1,131072]{2,1,0:T(1,128)} all-to-all(f32[4,1,131072]{2,1,0:T(1,128)S(1)} %reshape.97), channel_id=1, replica_groups=mesh['ax'=64,'az'=4] {'az'}, dimensions={0} | all-to-all | bytes 4194304 | tf_op jit(solution)/shard_map/all_to_all | solution.py:59
  357.1 0.5 broadcast.163
  357.7 7.7 %reduce = f32[4,131072]{1,0:T(4,128)S(1)} reduce(f32[4,1,131072]{2,1,0:T(1,128)} %all_to_all.103, f32[]{:T(128)} %broadcast.163), dimensions={1}, to_apply=%all_to_all.92.reduce_sub_computation | reduce | bytes 4194308 | tf_op jit(solution)/shard_map/all_to_all | solution.py:59
  365.4 3.9 %reshape.98 = f32[512,16,64]{2,1,0:T(8,128)} reshape(f32[4,131072]{1,0:T(4,128)S(1)} %reduce) | data formatting | bytes 4194304
  369.3 3.8 %copy.36 = f32[16,64,4,128]{3,1,2,0:T(8,128)} copy(f32[16,64,4,128]{1,0,3,2:T(8,128)} %bitcast.60) | data formatting | bytes 4194304 | tf_op jit(solution)/shard_map/all_to_all | solution.py:59
  373.1 0.0 copy-start.1
  373.1 5.9 %convolution_bitcast_fusion.1 = f32[16,256,128]{2,1,0:T(8,128)} fusion(f32[16,256,128]{2,1,0:T(8,128)} %bitcast.61, f32[256]{0:T(256)S(1)} %get-tuple-element.6, f32[256]{0:T(256)S(1)} %iota_multiply_fusion, f32[256]{0:T(256)S(1)} %get-tuple-element.5), kind=kOutput, calls=%fused_computation.23 | convolution fusion | flops 1610809344 | bytes 4197376 | tf_op jit(solution)/shard_map/xjy,mj->xmy/dot_general | solution.py:57
  379.0 0.0 copy-done.1
  (8 shorter events, 0.0 us)
Async XLA Ops:
  0.0 1.6 copy-start
  7.0 50.9 %all-to-all-start = ((f32[16,256,128]{2,0,1:T(8,128)}), f32[16,256,128]{2,0,1:T(8,128)S(1)}, u32[]{:S(2)}, u32[]{:S(2)}) async-start(f32[16,256,128]{2,0,1:T(8,128)} %copy.27), calls=%async_computation | async-start | bytes 4194304 | tf_op jit(solution)/shard_map/all_to_all | solution.py:40
  57.9 1.3 copy-start.2
  59.2 40.8 %all-to-all-start.2 = ((f32[16,256,128]{2,0,1:T(8,128)}), f32[16,256,128]{2,0,1:T(8,128)S(1)}, u32[]{:S(2)}, u32[]{:S(2)}) async-start(f32[16,256,128]{2,0,1:T(8,128)} %copy.31), calls=%async_computation.2 | async-start | bytes 4194304 | tf_op jit(solution)/shard_map/all_to_all | solution.py:41
  100.0 59.2 %all-to-all-start.1 = ((f32[16,64,512]{2,0,1:T(8,128)}), f32[16,64,512]{2,0,1:T(8,128)}, u32[]{:S(2)}, u32[]{:S(2)}) async-start(f32[16,64,512]{2,0,1:T(8,128)} %fusion.12), calls=%async_computation.1 | async-start | bytes 4194304 | tf_op jit(solution)/shard_map/all_to_all | solution.py:47
  159.2 34.8 %all-to-all-start.3 = ((f32[16,64,512]{2,0,1:T(8,128)}), f32[16,64,512]{2,0,1:T(8,128)}, u32[]{:S(2)}, u32[]{:S(2)}) async-start(f32[16,64,512]{2,0,1:T(8,128)} %fusion.10), calls=%async_computation.3 | async-start | bytes 4194304 | tf_op jit(solution)/shard_map/all_to_all | solution.py:48
  373.1 5.9 %copy-start.1 = (f32[16,256,128]{2,1,0:T(8,128)S(1)}, f32[16,256,128]{2,1,0:T(8,128)}, u32[]{:S(2)}) copy-start(f32[16,256,128]{2,1,0:T(8,128)} %param.2) | copy-start | bytes 6291460
where the time goes:
time: 387 us; the launch traced here: 379 us
  matrix products  120 us (31%)
  blocking collectives  86.4 us (22%)
  waiting for transfers between devices  64.6 us (17%)
  starting transfers between devices  54.7 us (14%)
  local copies, waits for them, and re-layouts  44.7 us (12%)
  other arithmetic  8.26 us (2%)
    all_to_all x1, blocking collectives, per_device(): lax.all_to_all(mixed, 'az', split_axis=2, concat_axis=1, tiled=True)  51.9 us
    dot_general x2, matrix products, per_device(): jnp.einsum('mry,mx->xry', field, axial, precision=highest)  51.7 us
    all_to_all x1, waiting for transfers between devices, per_device(): lax.all_to_all(state_radial, 'az', split_axis=1, concat_axis=2, tiled=True)  34.9 us
    all_to_all x1, blocking collectives, per_device(): lax.all_to_all(both_coeffs, 'ax', split_axis=0, concat_axis=1, tiled=True)  34.5 us
    all_to_all x1, starting transfers between devices, per_device(): lax.all_to_all(state_lines, 'ax', split_axis=1, concat_axis=0, tiled=True)  30 us
    dot_general x1, matrix products, per_device(): axial_coeffs = jnp.einsum('xry,mx->mry', weighted, axial, precision=highest)  24.5 us
    dot_general x2, matrix products, per_device(): jnp.einsum('xrm,my->xry', field, azimuth, precision=highest)  21.5 us
    unnamed x9, local copies, waits for them, and re-layouts  15.7 us
  transfers between devices with their start and end apart: 4, of which 4 were waited for; matrix products, arithmetic and copies ran while one was open for 16% of the time, Pallas kernels for 0%

commit v1 on v0

v1 whole, which is shorter than its diff:
```python
import functools
import math

import jax
import jax.numpy as jnp
import ml_dtypes
import numpy as np
from jax import lax
from jax.experimental import pallas as pl
from jax.experimental.pallas import tpu as pltpu
from jax.sharding import PartitionSpec as P

NX = 1024
NY = 512
NR = 256
BOTH = ("ax", "az")


def halves(table):
    high = table.astype(ml_dtypes.bfloat16)
    low = (table - high.astype(np.float64)).astype(ml_dtypes.bfloat16)
    return high, low


def fourier_table(count):
    modes = np.arange(count)[:, None]
    points = np.arange(count)[None, :]
    half = count // 2
    wave = np.where(modes <= half, modes, modes - half)
    angle = 2.0 * math.pi / count * (wave * points % count)
    scale = np.where((modes == 0) | (modes == half), math.sqrt(1.0 / count), math.sqrt(2.0 / count))
    return scale * np.where(modes <= half, np.cos(angle), np.sin(angle))


def radial_table(count):
    modes = np.arange(count)[:, None]
    points = np.arange(count)[None, :]
    weight = np.where(modes == 0, math.sqrt(1.0 / count), math.sqrt(2.0 / count))
    return weight * np.cos(math.pi * modes * (points + 0.5) / count)


def split(x):
    high = x.astype(jnp.bfloat16)
    low = (x - high.astype(jnp.float32)).astype(jnp.bfloat16)
    return high, low


def product(a, b, dims):
    dot = functools.partial(
        lax.dot_general, dimension_numbers=(dims, ((), ())), preferred_element_type=jnp.float32
    )
    return dot(a[0], b[0]) + (dot(a[0], b[1]) + dot(a[1], b[0]))


NN = ((1,), (0,))
NT = ((1,), (1,))


def radial_out(s_ref, a_ref, th_ref, tl_ref, out_ref):
    step = pl.program_id(0)
    table = th_ref[...], tl_ref[...]

    def synthesize(ref, group):
        for i in range(0, 8, 2):
            pair = jnp.concatenate([ref[i, 0], ref[i + 1, 0]], axis=1)
            result = product(table, split(pair), NN)
            out_ref[pl.ds(group * 8 + i, NR, stride=32), :] = result[:, :128]
            out_ref[pl.ds(group * 8 + i + 1, NR, stride=32), :] = result[:, 128:]

    for group in range(4):

        @pl.when(step == group)
        def _():
            synthesize(s_ref if group < 2 else a_ref, group)


def radial_back(in_ref, th_ref, tl_ref, out_ref):
    step = pl.program_id(0)
    table = th_ref[...], tl_ref[...]
    for parity in range(2):

        @pl.when(step == parity)
        def _():
            for i in range(0, 8, 2):
                row = parity * 8 + i
                pair = jnp.concatenate(
                    [in_ref[pl.ds(row, NR, stride=16), :], in_ref[pl.ds(row + 1, NR, stride=16), :]],
                    axis=1,
                )
                result = product(table, split(pair), NN)
                out_ref[i, 0] = result[:, :128]
                out_ref[i + 1, 0] = result[:, 128:]


def grid_kernel(
    in_ref, yh_ref, yl_ref, eh_ref, el_ref, oh_ref, ol_ref, pth_ref, ptl_ref, out_ref,
    high_ref, low_ref, state_ref, work_ref,
):
    half = NX // 2
    root = math.sqrt(0.5)

    def synthesis(field):
        for chunk in range(2):
            parts = []
            for parity in range(2):
                lanes = [
                    in_ref[:, 2 * chunk + k, field, parity].reshape(half, 128) for k in range(2)
                ]
                x = split(jnp.concatenate(lanes, axis=1))
                table = (eh_ref, el_ref) if parity == 0 else (oh_ref, ol_ref)
                parts.append(product((table[0][...], table[1][...]), x, NN))
            even, odd = parts
            columns = pl.ds(256 * chunk, 256)
            for k, value in enumerate((even + odd, even - odd)):
                high, low = split(value)
                high_ref[pl.ds(half * k, half), columns] = high
                low_ref[pl.ds(half * k, half), columns] = low

    def azimuth_synthesis(rows):
        lines = high_ref[rows, :], low_ref[rows, :]
        return product(lines, (yh_ref[...], yl_ref[...]), NN)

    synthesis(0)

    @pl.loop(0, 4)
    def _(i):
        rows = pl.ds(pl.multiple_of(i * 256, 256), 256)
        state_ref[rows, :] = azimuth_synthesis(rows)

    synthesis(1)

    @pl.loop(0, 4)
    def _(i):
        rows = pl.ds(pl.multiple_of(i * 256, 256), 256)
        state = state_ref[rows, :]
        work_ref[rows, :] = (3.0 * state * state - 1.0) * azimuth_synthesis(rows)

    for chunk in range(2):
        columns = pl.ds(256 * chunk, 256)
        first = work_ref[pl.ds(0, half), columns]
        second = work_ref[pl.ds(half, half), columns]
        even = product((yh_ref[...], yl_ref[...]), split((first + second) * root), NN)
        odd = product((pth_ref[...], ptl_ref[...]), split(first - second), NN)
        for k, value in enumerate((even, odd)):
            high, low = split(value)
            high_ref[pl.ds(half * k, half), columns] = high
            low_ref[pl.ds(half * k, half), columns] = low

    for parity in range(2):

        @pl.loop(0, 2)
        def _(i):
            rows = pl.ds(pl.multiple_of(parity * half + i * 256, 256), 256)
            lines = high_ref[rows, :], low_ref[rows, :]
            result = product(lines, (yh_ref[...], yl_ref[...]), NT)
            for k in range(4):
                block = result[:, 128 * k : 128 * (k + 1)].reshape(32, 8, 128)
                out_ref[pl.ds(pl.multiple_of(i * 32, 32), 32), k, parity] = block


def whole():
    return pl.BlockSpec(memory_space=pltpu.VMEM)


def params(**more):
    return pltpu.CompilerParams(vmem_limit_bytes=56 * 2**20, **more)


def per_device(phase_field, section_cotangent):
    radial = radial_table(NR)
    azimuth = fourier_table(NY)
    axial = fourier_table(NX)
    ch, cl = halves(radial)
    cth, ctl = halves(np.ascontiguousarray(radial.T))
    yh, yl = halves(azimuth)
    eh, el = halves(np.ascontiguousarray(axial[0::2, : NX // 2].T))
    ph, plow = halves(np.ascontiguousarray(axial[1::2, : NX // 2].T))
    pth, ptl = halves(np.ascontiguousarray(axial[1::2, : NX // 2]))

    s = phase_field.reshape(8, 2, NR, 128)
    a = section_cotangent.reshape(8, 2, NR, 128)
    table_spec = pl.BlockSpec((NR, NR), lambda g: (0, 0))
    sent = pl.pallas_call(
        radial_out,
        grid=(4,),
        in_specs=[
            pl.BlockSpec((8, 1, NR, 128), lambda g: (0, jnp.minimum(g, 1), 0, 0)),
            pl.BlockSpec((8, 1, NR, 128), lambda g: (0, jnp.maximum(g - 2, 0), 0, 0)),
            table_spec,
            table_spec,
        ],
        out_specs=pl.BlockSpec((NR * 32, 128), lambda g: (0, 0)),
        out_shape=jax.ShapeDtypeStruct((NR * 32, 128), jnp.float32),
        compiler_params=params(),
        name="radial_out",
    )(s, a, cth, ctl)
    taken = lax.all_to_all(sent.reshape(NR, 32, 128), BOTH, split_axis=0, concat_axis=0, tiled=True)
    weighted = pl.pallas_call(
        grid_kernel,
        in_specs=[whole()] * 9,
        out_specs=whole(),
        out_shape=jax.ShapeDtypeStruct((64, 4, 2, 8, 128), jnp.float32),
        scratch_shapes=[
            pltpu.VMEM((NX, NY), jnp.bfloat16),
            pltpu.VMEM((NX, NY), jnp.bfloat16),
            pltpu.VMEM((NX, NY), jnp.float32),
            pltpu.VMEM((NX, NY), jnp.float32),
        ],
        compiler_params=params(),
        name="grid",
    )(taken.reshape(64, 4, 2, 2, 8, 128), yh, yl, eh, el, ph, plow, pth, ptl)
    back = lax.all_to_all(weighted.reshape(NR, 16, 128), BOTH, split_axis=0, concat_axis=0, tiled=True)
    gradient = pl.pallas_call(
        radial_back,
        grid=(2,),
        in_specs=[pl.BlockSpec((NR * 16, 128), lambda g: (0, 0)), table_spec, table_spec],
        out_specs=pl.BlockSpec((8, 1, NR, 128), lambda g: (0, g, 0, 0)),
        out_shape=jax.ShapeDtypeStruct((8, 2, NR, 128), jnp.float32),
        compiler_params=params(),
        name="radial_back",
    )(back.reshape(NR * 16, 128), ch, cl)
    return gradient.reshape(16, NR, 128)


def solution(mesh):
    spec = P("ax", None, "az")
    return jax.shard_map(
        per_device, mesh=mesh, in_specs=(spec, spec), out_specs=spec, check_vma=False
    )
```

time: 387 us -> 207 us (0.53); the launches traced: 379 us -> 207 us
  matrix products: 120 us -> 0 us
  blocking collectives: 86.4 us -> 178 us
  waiting for transfers between devices: 64.6 us -> 0 us
  starting transfers between devices: 54.7 us -> 0 us
  local copies, waits for them, and re-layouts: 44.7 us -> 0 us
  Pallas kernels: 0 us -> 29.5 us
  other arithmetic: 8.26 us -> 0 us
    dot_general x9 -> x0, matrix products: 120 us -> none  [the longest x2 51.7 us: per_device(): jnp.einsum('mry,mx->xry', field, axial, precision=highest)]
    all_to_all x2, blocking collectives: 86.4 us -> 178 us  [the longest x1 116 us: per_device(): lax.all_to_all(sent.reshape(NR, 32, 128), BOTH, split_axis=0, concat_axis...]
    all_to_all x4 -> x0, waiting for transfers between devices: 64.6 us -> none  [the longest x1 34.9 us: per_device(): lax.all_to_all(state_radial, 'az', split_axis=1, concat_axis=2, tiled=True)]
    all_to_all x4 -> x0, starting transfers between devices: 54.7 us -> none  [the longest x1 30 us: per_device(): lax.all_to_all(state_lines, 'ax', split_axis=1, concat_axis=0, tiled=True)]
    pallas_call x0 -> x3, Pallas kernels: none -> 29.5 us  [the longest x1 17.2 us: per_device(): pl.pallas_call(grid_kernel, in_specs=[whole()] * 9, out_specs=whole(), ou...]
    all_to_all x7 -> x0, local copies, waits for them, and re-layouts: 21.7 us -> none  [the longest x2 7.35 us: per_device(): lax.all_to_all(state_radial, 'az', split_axis=1, concat_axis=2, tiled=True)]
    unnamed x9 -> x0, local copies, waits for them, and re-layouts: 15.7 us -> none
    all_to_all x1 -> x0, other arithmetic: 7.72 us -> none  [per_device(): lax.all_to_all(mixed, 'az', split_axis=2, concat_axis=1, tiled=True)]
  transfers between devices with their start and end apart: 4 -> 0, of which waited for: 4 -> 0; matrix products, arithmetic and copies ran while one was open for 16% -> 0% of each run, Pallas kernels for 0% -> 0%
where the time goes in v1:
time: 207 us
  blocking collectives  178 us (86%)
  Pallas kernels  29.5 us (14%)
    all_to_all x1, blocking collectives, per_device(): lax.all_to_all(sent.reshape(NR, 32, 128), BOTH, split_axis=0, concat_axis...  116 us
    all_to_all x1, blocking collectives, per_device(): lax.all_to_all(weighted.reshape(NR, 16, 128), BOTH, split_axis=0, concat_...  61.8 us
    pallas_call x1, Pallas kernels, per_device(): pl.pallas_call(grid_kernel, in_specs=[whole()] * 9, out_specs=whole(), ou...  17.2 us
    pallas_call x1, Pallas kernels, per_device(): pl.pallas_call(radial_out, grid=(4,), in_specs=[pl.BlockSpec((8, 1, NR, 1...  7.97 us
    pallas_call x1, Pallas kernels, per_device(): pl.pallas_call(radial_back, grid=(2,), in_specs=[pl.BlockSpec((NR * 16, 1...  4.38 us

profile of v1, /device:TPU:1, one launch (start us, length us, event | category | flops | bytes accessed | tf_op | source)
XLA Modules:
  0.0 207.1 jit_solution(8229327096862848404)
XLA Ops:
  0.0 8.0 %radial_out.1 = f32[8192,128]{1,0:T(8,128)} custom-call(f32[8,2,256,128]{3,2,1,0:T(8,128)} %bitcast.11, f32[8,2,256,128]{3,2,1,0:T(8,128)} %bitcast.12, bf16[256,256]{1,0:T(8,128)(2,1)} %constant.24.clone.th_ref, bf16[256,256]{1,0:T(8,128)(2,1)} %constant.25.clone.tl_ref), custom_call_target="tpu_custom_call" | custom-call | tf_op jit(solution)/shard_map/radial_out/pallas_call | solution.py:183
  8.0 115.8 %all_to_all.10 = f32[256,32,128]{2,1,0:T(8,128)} all-to-all(f32[256,32,128]{2,1,0:T(8,128)} %bitcast.8), channel_id=1, replica_groups=mesh['ax'=64,'az'=4] {'ax','az'}, dimensions={0} | all-to-all | bytes 8388608 | tf_op jit(solution)/shard_map/all_to_all | solution.py:197
  123.8 17.2 %grid.1 = f32[64,4,2,8,128]{4,3,2,1,0:T(8,128)} custom-call(f32[64,4,2,2,8,128]{5,4,3,2,1,0:T(8,128)} %bitcast.7, bf16[512,512]{1,0:T(8,128)(2,1)} %constant.26.clone.yh_ref, bf16[512,512]{1,0:T(8,128)(2,1)} %constant.27.clone.yl_ref, bf16[512,512]{1,0:T(8,128)(2,1)} %constant.28.clone.eh_ref, bf16[512,512]{1,0:T(8,128)(2,1)} %constant.29.clone.el_ref, ...), custom_call_target="tpu_custom_call" | custom-call | tf_op jit(solution)/shard_map/grid/pallas_call | solution.py:198
  141.0 61.8 %all_to_all.11 = f32[256,16,128]{2,1,0:T(8,128)} all-to-all(f32[256,16,128]{2,1,0:T(8,128)} %bitcast.9), channel_id=1, replica_groups=mesh['ax'=64,'az'=4] {'ax','az'}, dimensions={0} | all-to-all | bytes 4194304 | tf_op jit(solution)/shard_map/all_to_all | solution.py:212
  202.8 4.4 %radial_back.1 = f32[8,2,256,128]{3,2,1,0:T(8,128)} custom-call(f32[4096,128]{1,0:T(8,128)} %bitcast.10, bf16[256,256]{1,0:T(8,128)(2,1)} %constant.34.clone.th_ref, bf16[256,256]{1,0:T(8,128)(2,1)} %constant.35.clone.tl_ref), custom_call_target="tpu_custom_call" | custom-call | tf_op jit(solution)/shard_map/radial_back/pallas_call | solution.py:213

commit v2 on v0

v2 whole, which is shorter than its diff:
```python
import functools
import math

import jax
import jax.numpy as jnp
import ml_dtypes
import numpy as np
from jax import lax
from jax.experimental import pallas as pl
from jax.experimental.pallas import tpu as pltpu
from jax.sharding import Mesh, PartitionSpec as P

NX = 1024
NY = 512
NR = 256
AXES = ("x", "y", "zl", "co", "zh")
SHARD = ("x", "y", "zl", "co")
RING = ("zl", "zh")
PLANE = ("x", "y", "co")
OFFSETS = (3, 5, 4, 2, 6, 1, 7)


def halves(table):
    high = table.astype(ml_dtypes.bfloat16)
    low = (table - high.astype(np.float64)).astype(ml_dtypes.bfloat16)
    return high, low


def fourier_table(count):
    modes = np.arange(count)[:, None]
    points = np.arange(count)[None, :]
    half = count // 2
    wave = np.where(modes <= half, modes, modes - half)
    angle = 2.0 * math.pi / count * (wave * points % count)
    scale = np.where((modes == 0) | (modes == half), math.sqrt(1.0 / count), math.sqrt(2.0 / count))
    return scale * np.where(modes <= half, np.cos(angle), np.sin(angle))


def radial_table(count):
    modes = np.arange(count)[:, None]
    points = np.arange(count)[None, :]
    weight = np.where(modes == 0, math.sqrt(1.0 / count), math.sqrt(2.0 / count))
    return weight * np.cos(math.pi * modes * (points + 0.5) / count)


def split(x):
    high = x.astype(jnp.bfloat16)
    low = (x - high.astype(jnp.float32)).astype(jnp.bfloat16)
    return high, low


def product(a, b, dims):
    dot = functools.partial(
        lax.dot_general, dimension_numbers=(dims, ((), ())), preferred_element_type=jnp.float32
    )
    return dot(a[0], b[0]) + (dot(a[0], b[1]) + dot(a[1], b[0]))


NN = ((1,), (0,))
NT = ((1,), (1,))


def my_z():
    return 2 * lax.axis_index("zh") + lax.axis_index("zl")


def radial_out(ring_first, z_ref, x_ref, th_ref, tl_ref, *out_refs):
    group = pl.program_id(0)
    rows = pl.ds(pl.multiple_of(z_ref[0] * 32, 32), NR)
    table = th_ref[rows, :], tl_ref[rows, :]
    for i in range(0, 8, 2):
        pair = jnp.concatenate([x_ref[i, 0], x_ref[i + 1, 0]], axis=1)
        result = product(table, split(pair), NN)
        for k in range(2):
            for o in range(8):
                value = result[32 * o : 32 * (o + 1), 128 * k : 128 * (k + 1)]
                row = group * 8 + i + k
                if ring_first:
                    out_refs[o][pl.ds(row, 32, stride=16), :] = value
                else:
                    out_refs[0][pl.ds(16 * o + row, 32, stride=128), :] = value


def merge(*refs):
    for o in range(8):
        refs[8][:, o] = refs[o][...]


def spread(in_ref, *out_refs):
    for o in range(8):
        out_refs[o][...] = in_ref[:, o]


def place(z, value_of, high_ref, low_ref):
    for o in range(8):
        source = lax.rem(z - o + 8, 8)
        rows = pl.ds(pl.multiple_of(lax.rem(source, 2) * 16, 16), 16)
        columns = pl.ds(pl.multiple_of(lax.div(source, 2) * 128, 128), 128)
        for parity in range(2):
            high, low = split(value_of(o, parity).reshape(16, 16, 128))
            high_ref[parity, :, rows, columns] = high
            low_ref[parity, :, rows, columns] = low


def axial_synthesis(xh_ref, xl_ref, tables, high_ref, low_ref):
    half = NX // 2
    for chunk in range(2):
        columns = pl.ds(256 * chunk, 256)
        parts = []
        for parity in range(2):
            th_ref, tl_ref = tables[parity]
            x = [ref[parity, :, :, columns].reshape(half, 256) for ref in (xh_ref, xl_ref)]
            parts.append(product((th_ref[...], tl_ref[...]), x, NN))
        even, odd = parts
        for k, value in enumerate((even + odd, even - odd)):
            high, low = split(value)
            high_ref[pl.ds(half * k, half), columns] = high
            low_ref[pl.ds(half * k, half), columns] = low


def state_kernel(
    z_ref, in_ref, yh_ref, yl_ref, eh_ref, el_ref, oh_ref, ol_ref, state_ref,
    xh_ref, xl_ref, high_ref, low_ref,
):
    place(z_ref[0], lambda o, parity: in_ref[:, o, parity], xh_ref, xl_ref)
    axial_synthesis(xh_ref, xl_ref, ((eh_ref, el_ref), (oh_ref, ol_ref)), high_ref, low_ref)

    @pl.loop(0, 4)
    def _(i):
        rows = pl.ds(pl.multiple_of(i * 256, 256), 256)
        lines = high_ref[rows, :], low_ref[rows, :]
        state_ref[rows, :] = product(lines, (yh_ref[...], yl_ref[...]), NN)


def analysis(z, table, folded, azimuth, store, high_ref, low_ref, result_ref):
    for chunk in range(2):
        value = product(table, folded(pl.ds(256 * chunk, 256)), NN)
        high, low = split(value)
        columns = pl.ds(256 * chunk, 256)
        high_ref[:, columns] = high
        low_ref[:, columns] = low

    @pl.loop(0, 2)
    def _(i):
        rows = pl.ds(pl.multiple_of(i * 256, 256), 256)
        value = product((high_ref[rows, :], low_ref[rows, :]), azimuth, NT)
        result_ref[pl.ds(pl.multiple_of(i * 8, 8), 8)] = value.reshape(8, 2, 16, NY)

    for o in range(8):
        target = lax.rem(z + o, 8)
        columns = pl.ds(pl.multiple_of(lax.div(target, 2) * 128, 128), 128)
        store(o, result_ref[:, lax.rem(target, 2), :, columns].reshape(32, 8, 128))


def grid_kernel(
    z_ref, state_ref, p0, p1, p2, p3, p4, p5, p6, p7,
    yh_ref, yl_ref, eh_ref, el_ref, oh_ref, ol_ref,
    q0, q1, q2, q3, q4, q5, q6, q7, odd_h_ref, odd_l_ref,
    xh_ref, xl_ref, high_ref, low_ref, work_ref, result_ref,
):
    pieces = (p0, p1, p2, p3, p4, p5, p6, p7)
    outs = (q0, q1, q2, q3, q4, q5, q6, q7)
    half = NX // 2
    place(z_ref[0], lambda o, parity: pieces[o][:, parity], xh_ref, xl_ref)
    axial_synthesis(xh_ref, xl_ref, ((eh_ref, el_ref), (oh_ref, ol_ref)), high_ref, low_ref)
    azimuth = yh_ref[...], yl_ref[...]

    @pl.loop(0, 4)
    def _(i):
        rows = pl.ds(pl.multiple_of(i * 256, 256), 256)
        state = state_ref[rows, :]
        adjoint = product((high_ref[rows, :], low_ref[rows, :]), azimuth, NN)
        work_ref[rows, :] = (3.0 * state * state - 1.0) * adjoint

    first, second = pl.ds(0, half), pl.ds(half, half)
    odd_h_ref[...], odd_l_ref[...] = split(work_ref[first, :] - work_ref[second, :])
    root = math.sqrt(0.5)

    def store(o, value):
        outs[o][...] = value

    analysis(
        z_ref[0], azimuth,
        lambda c: split((work_ref[first, c] + work_ref[second, c]) * root), azimuth, store,
        high_ref.at[first], low_ref.at[first], result_ref,
    )


def odd_kernel(
    z_ref, odd_h_ref, odd_l_ref, yh_ref, yl_ref, ph_ref, pl_ref, out_ref, high_ref, low_ref, result_ref
):
    def store(o, value):
        out_ref[:, o] = value

    analysis(
        z_ref[0], (ph_ref[...], pl_ref[...]), lambda c: (odd_h_ref[:, c], odd_l_ref[:, c]),
        (yh_ref[...], yl_ref[...]), store, high_ref, low_ref, result_ref,
    )


def radial_back(merged, z_ref, th_ref, tl_ref, *refs):
    in_refs, (out_ref, high_ref, low_ref) = refs[: 1 if merged else 8], refs[-3:]
    table = th_ref[...], tl_ref[...]
    for i in range(0, 8, 2):
        for o in range(8):
            rows = pl.ds(pl.multiple_of(lax.rem(z_ref[0] - o + 8, 8) * 32, 32), 32)
            for k in range(2):
                if merged:
                    value = in_refs[0][pl.ds(8 * o + i + k, 32, stride=64), :]
                else:
                    value = in_refs[o][pl.ds(i + k, 32, stride=8), :]
                columns = slice(128 * k, 128 * (k + 1))
                high_ref[i // 2, rows, columns], low_ref[i // 2, rows, columns] = split(value)
    for i in range(0, 8, 2):
        result = product(table, (high_ref[i // 2], low_ref[i // 2]), NN)
        out_ref[i, 0] = result[:, :128]
        out_ref[i + 1, 0] = result[:, 128:]


def call(kernel, name, outs, ins, flops=0, scratch=(), **more):
    vmem = pl.BlockSpec(memory_space=pltpu.VMEM)
    size = sum(math.prod(a.shape) * a.dtype.itemsize for a in (*ins[1:], *outs))
    return pl.pallas_call(
        kernel,
        in_specs=more.pop("in_specs", [pl.BlockSpec(memory_space=pltpu.SMEM)] + [vmem] * (len(ins) - 1)),
        out_specs=more.pop("out_specs", [vmem] * len(outs)),
        out_shape=outs,
        scratch_shapes=list(scratch),
        cost_estimate=pl.CostEstimate(flops=flops, bytes_accessed=size, transcendentals=0),
        compiler_params=pltpu.CompilerParams(vmem_limit_bytes=LIMIT),
        name=name,
        **more,
    )(*ins)


LIMIT = 40 * 2**20


def f32(*shape):
    return jax.ShapeDtypeStruct(shape, jnp.float32)


def bf16(*shape):
    return jax.ShapeDtypeStruct(shape, jnp.bfloat16)


def ring_index(z):
    return (z % 2) * 4 + (z % 8) // 2


def ring(pieces):
    out = list(pieces)
    for o in OFFSETS:
        pairs = [(ring_index(z), ring_index(z + o)) for z in range(8)]
        out[o] = lax.ppermute(pieces[o], RING, pairs)
    return out


def plane(x):
    return lax.all_to_all(x, PLANE, split_axis=0, concat_axis=0, tiled=True)


def per_device(phase_field, section_cotangent):
    radial = radial_table(NR)
    axial = fourier_table(NX)
    c = halves(radial)
    ct = halves(np.concatenate([radial.T, radial.T]))
    y = halves(fourier_table(NY))
    e = halves(np.ascontiguousarray(axial[0::2, : NX // 2].T))
    p = halves(np.ascontiguousarray(axial[1::2, : NX // 2].T))
    pt = halves(np.ascontiguousarray(axial[1::2, : NX // 2]))
    z = my_z().astype(jnp.int32).reshape(1)
    point = 2 * 3

    def synthesize(x, ring_first, name):
        outs = [f32(512, 128)] * 8 if ring_first else [f32(4096, 128)]
        table = pl.BlockSpec((2 * NR, NR), lambda g: (0, 0))
        return call(
            functools.partial(radial_out, ring_first), name, outs,
            [z, x.reshape(8, 2, NR, 128), *ct], point * NR * 2**19, grid=(2,),
            in_specs=[
                pl.BlockSpec(memory_space=pltpu.SMEM),
                pl.BlockSpec((8, 1, NR, 128), lambda g: (0, g, 0, 0)), table, table,
            ],
            out_specs=[pl.BlockSpec(o.shape, lambda g: (0, 0)) for o in outs],
        )

    s = synthesize(phase_field, True, "radial_state")
    s = ring(s)
    (a,) = synthesize(section_cotangent, False, "radial_adjoint")
    a = plane(a.reshape(32, 8, 16, 128))
    a = pl.pallas_call(
        spread, in_specs=[pl.BlockSpec(memory_space=pltpu.VMEM)],
        out_specs=[pl.BlockSpec(memory_space=pltpu.VMEM)] * 8, out_shape=[f32(32, 16, 128)] * 8,
        name="spread_adjoint",
    )(a)
    a = ring(a)

    def merged(pieces, name):
        rows = pieces[0].shape[1]
        return pl.pallas_call(
            merge, in_specs=[pl.BlockSpec(memory_space=pltpu.VMEM)] * 8,
            out_specs=pl.BlockSpec(memory_space=pltpu.VMEM), out_shape=f32(32, 8, rows, 128), name=name,
        )(*pieces)

    s = plane(merged([v.reshape(32, 16, 128) for v in s], "merge_state"))
    places = [pltpu.VMEM((2, 16, 32, NY), jnp.bfloat16)] * 2
    lines = [pltpu.VMEM((NX, NY), jnp.bfloat16)] * 2
    small = [pltpu.VMEM((NX // 2, NY), jnp.bfloat16)] * 2
    result = pltpu.VMEM((16, 2, 16, NY), jnp.float32)
    (state,) = call(
        state_kernel, "state", [f32(NX, NY)], [z, s.reshape(32, 8, 2, 8, 128), *y, *e, *p],
        point * 1024 * 2**19, scratch=places + lines,
    )
    *even, odd_h, odd_l = call(
        grid_kernel, "grid", [f32(32, 8, 128)] * 8 + [bf16(NX // 2, NY)] * 2,
        [z, state, *(v.reshape(32, 2, 8, 128) for v in a), *y, *e, *p], point * 1536 * 2**19,
        scratch=places + lines + [pltpu.VMEM((NX, NY), jnp.float32), result],
    )
    even = ring(even)
    (odd,) = call(
        odd_kernel, "odd", [f32(32, 8, 8, 128)], [z, odd_h, odd_l, *y, *pt], point * 512 * 2**19,
        scratch=small + [result],
    )
    odd = plane(odd)
    odd = pl.pallas_call(
        spread, in_specs=[pl.BlockSpec(memory_space=pltpu.VMEM)],
        out_specs=[pl.BlockSpec(memory_space=pltpu.VMEM)] * 8, out_shape=[f32(32, 8, 128)] * 8,
        name="spread_odd",
    )(odd)
    odd = ring(odd)
    even = plane(merged(even, "merge_even"))

    def back(pieces, parity, before, name):
        ins = [z, *c, *pieces]
        vmem = pl.BlockSpec(memory_space=pltpu.VMEM)
        specs = [pl.BlockSpec(memory_space=pltpu.SMEM)] + [vmem] * (len(ins) - 1)
        kernel = functools.partial(radial_back, len(pieces) == 1)
        more = {}
        if before is not None:
            body, count = kernel, len(ins)
            kernel = lambda *refs: body(*refs[:count], *refs[count + 1 :])
            more = {"input_output_aliases": {count: 0}}
            ins.append(before)
            specs.append(pl.BlockSpec(memory_space=pl.ANY))
        return call(
            kernel, name, [f32(8, 2, NR, 128)], ins, point * 128 * 2**19, grid=(1,),
            in_specs=specs,
            out_specs=[pl.BlockSpec((8, 1, NR, 128), lambda g: (0, parity, 0, 0))],
            scratch=[pltpu.VMEM((4, NR, 256), jnp.bfloat16)] * 2, **more,
        )[0]

    out = back([even.reshape(2048, 128)], 0, None, "radial_even")
    out = back([v.reshape(256, 128) for v in odd], 1, out, "radial_odd")
    return out.reshape(16, NR, 128)


def solution(mesh):
    names = Mesh(mesh.devices.reshape(4, 4, 2, 2, 4), AXES)
    spec = P(SHARD, None, "zh")
    return jax.shard_map(
        per_device, mesh=names, in_specs=(spec, spec), out_specs=spec, check_vma=False
    )
```

time: 387 us -> 246 us (0.64); the launches traced: 379 us -> 245 us
  matrix products: 120 us -> 0 us
  blocking collectives: 86.4 us -> 0 us
  waiting for transfers between devices: 64.6 us -> 103 us
  starting transfers between devices: 54.7 us -> 92.3 us
  Pallas kernels: 0 us -> 36.6 us
  local copies, waits for them, and re-layouts: 44.7 us -> 12.5 us
  other arithmetic: 8.26 us -> 0 us
    dot_general x9 -> x0, matrix products: 120 us -> none  [the longest x2 51.7 us: per_device(): jnp.einsum('mry,mx->xry', field, axial, precision=highest)]
    ppermute x0 -> x28, waiting for transfers between devices: none -> 99.5 us  [ring(): out[o] = lax.ppermute(pieces[o], RING, pairs)]
    all_to_all x2 -> x0, blocking collectives: 86.4 us -> none  [the longest x1 51.9 us: per_device(): lax.all_to_all(mixed, 'az', split_axis=2, concat_axis=1, tiled=True)]
    all_to_all x4, waiting for transfers between devices: 64.6 us -> 3.74 us  [plane(): return lax.all_to_all(x, PLANE, split_axis=0, concat_axis=0, tiled=True)]
    ppermute x0 -> x28, starting transfers between devices: none -> 59.4 us  [ring(): out[o] = lax.ppermute(pieces[o], RING, pairs)]
    pallas_call x0 -> x11, Pallas kernels: none -> 36.6 us  [the longest x7 26 us: call(): pl.pallas_call(kernel, in_specs=more.pop('in_specs', [pl.BlockSpec(memory...]
    all_to_all x4, starting transfers between devices: 54.7 us -> 32.9 us  [plane(): return lax.all_to_all(x, PLANE, split_axis=0, concat_axis=0, tiled=True)]
    all_to_all x7 -> x0, local copies, waits for them, and re-layouts: 21.7 us -> none  [the longest x2 7.35 us: per_device(): lax.all_to_all(state_radial, 'az', split_axis=1, concat_axis=2, tiled=True)]
  transfers between devices with their start and end apart: 4 -> 32, of which waited for: 4 -> 20; matrix products, arithmetic and copies ran while one was open for 16% -> 0% of each run, Pallas kernels for 0% -> 8%
where the time goes in v2:
time: 246 us; the launch traced here: 245 us
  waiting for transfers between devices  103 us (42%)
  starting transfers between devices  92.3 us (38%)
  Pallas kernels  36.6 us (15%)
  local copies, waits for them, and re-layouts  12.5 us (5%)
    ppermute x28, waiting for transfers between devices, ring(): out[o] = lax.ppermute(pieces[o], RING, pairs)  99.5 us
    ppermute x28, starting transfers between devices, ring(): out[o] = lax.ppermute(pieces[o], RING, pairs)  59.4 us
    all_to_all x4, starting transfers between devices, plane(): return lax.all_to_all(x, PLANE, split_axis=0, concat_axis=0, tiled=True)  32.9 us
    pallas_call x7, Pallas kernels, call(): pl.pallas_call(kernel, in_specs=more.pop('in_specs', [pl.BlockSpec(memory...  26 us
    unnamed x82, local copies, waits for them, and re-layouts  12.5 us
    pallas_call x2, Pallas kernels, merged(): pl.pallas_call(merge, in_specs=[pl.BlockSpec(memory_space=pltpu.VMEM)] *...  5.36 us
    pallas_call x2, Pallas kernels, per_device(): pl.pallas_call(spread, in_specs=[pl.BlockSpec(memory_space=pltpu.VMEM)],...  5.24 us
  transfers between devices with their start and end apart: 32, of which 20 were waited for; matrix products, arithmetic and copies ran while one was open for 0% of the time, Pallas kernels for 8%

profile of v2, /device:TPU:1, one launch (start us, length us, event | category | flops | bytes accessed | tf_op | source)
XLA Modules:
  0.0 244.9 jit_solution(16169328422146180006)
XLA Ops:
  0.0 1.6 copy-done
  1.6 0.9 copy-done.4
  2.5 0.9 copy-done.6
  3.5 3.6 %radial_adjoint.1 = f32[4096,128]{1,0:T(8,128)} custom-call(s32[1]{0:T(128)} %bitcast.z_ref.refs_0_, f32[8,2,256,128]{3,2,1,0:T(8,128)S(1)} %bitcast.32, bf16[512,256]{1,0:T(8,128)(2,1)S(1)} %copy-done.6, bf16[512,256]{1,0:T(8,128)(2,1)S(1)} %copy-done.4), custom_call_target="tpu_custom_call" | custom-call | flops 805306368 | bytes 4718592 | tf_op jit(solution)/shard_map/radial_adjoint/pallas_call | solution.py:223
  7.1 8.9 %all-to-all-start.1 = ((f32[32,8,16,128]{3,2,1,0:T(8,128)}), f32[32,8,16,128]{3,2,1,0:T(8,128)}, u32[]{:S(2)}, u32[]{:S(2)}) async-start(f32[32,8,16,128]{3,2,1,0:T(8,128)} %bitcast.12), calls=%async_computation.1 | async-start | bytes 4194304 | tf_op jit(solution)/shard_map/all_to_all | solution.py:260
  16.0 1.7 radial_state.1
  17.7 0.7 copy-done.3
  18.5 1.6 collective-permute-start
  20.1 3.0 %collective-permute-start.1 = (f32[512,128]{1,0:T(8,128)S(1)}, f32[512,128]{1,0:T(8,128)S(1)}, u32[]{:S(2)}, u32[]{:S(2)}) collective-permute-start(f32[512,128]{1,0:T(8,128)S(1)} %get-tuple-element.41), channel_id=1, source_target_pairs={{0,1},{8,9},{1,2},{9,10},{2,3},{10,11},{3,0},{11,8},{4,5},{12,13},... | collective-permute-start | bytes 786440 | tf_op jit(solution)/shard_map/ppermute | solution.py:255
  23.1 3.8 %collective-permute-start.2 = (f32[512,128]{1,0:T(8,128)S(1)}, f32[512,128]{1,0:T(8,128)S(1)}, u32[]{:S(2)}, u32[]{:S(2)}) collective-permute-start(f32[512,128]{1,0:T(8,128)S(1)} %get-tuple-element.42), channel_id=1, source_target_pairs={{0,9},{8,2},{1,10},{9,3},{2,11},{10,0},{3,8},{11,1},{4,13},{12,6},... | collective-permute-start | bytes 786440 | tf_op jit(solution)/shard_map/ppermute | solution.py:255
  27.3 4.5 %collective-permute-start.4 = (f32[512,128]{1,0:T(8,128)S(1)}, f32[512,128]{1,0:T(8,128)S(1)}, u32[]{:S(2)}, u32[]{:S(2)}) collective-permute-start(f32[512,128]{1,0:T(8,128)S(1)} %get-tuple-element.44), channel_id=1, source_target_pairs={{0,10},{8,3},{1,11},{9,0},{2,8},{10,1},{3,9},{11,2},{4,14},{12,7},... | collective-permute-start | bytes 786440 | tf_op jit(solution)/shard_map/ppermute | solution.py:255
  31.8 2.4 collective-permute-start.5
  34.2 3.5 %collective-permute-done.1 = f32[512,128]{1,0:T(8,128)S(1)} collective-permute-done((f32[512,128]{1,0:T(8,128)S(1)}, f32[512,128]{1,0:T(8,128)S(1)}, u32[]{:S(2)}, u32[]{:S(2)}) %collective-permute-start.1) | collective-permute-done | bytes 262176 | tf_op jit(solution)/shard_map/ppermute | solution.py:255
  37.7 6.7 %collective-permute-start.6 = (f32[512,128]{1,0:T(8,128)S(1)}, f32[512,128]{1,0:T(8,128)S(1)}, u32[]{:S(2)}, u32[]{:S(2)}) collective-permute-start(f32[512,128]{1,0:T(8,128)S(1)} %get-tuple-element.46), channel_id=1, source_target_pairs={{0,11},{8,0},{1,8},{9,1},{2,9},{10,2},{3,10},{11,3},{4,15},{12,4},... | collective-permute-start | bytes 786440 | tf_op jit(solution)/shard_map/ppermute | solution.py:255
  44.4 14.6 %collective-permute-done.2 = f32[512,128]{1,0:T(8,128)S(1)} collective-permute-done((f32[512,128]{1,0:T(8,128)S(1)}, f32[512,128]{1,0:T(8,128)S(1)}, u32[]{:S(2)}, u32[]{:S(2)}) %collective-permute-start.2) | collective-permute-done | bytes 262176 | tf_op jit(solution)/shard_map/ppermute | solution.py:255
  59.0 4.8 %collective-permute-done.3 = f32[512,128]{1,0:T(8,128)S(1)} collective-permute-done((f32[512,128]{1,0:T(8,128)S(1)}, f32[512,128]{1,0:T(8,128)S(1)}, u32[]{:S(2)}, u32[]{:S(2)}) %collective-permute-start.3) | collective-permute-done | bytes 262176 | tf_op jit(solution)/shard_map/ppermute | solution.py:255
  63.9 7.7 %collective-permute-done.5 = f32[512,128]{1,0:T(8,128)S(1)} collective-permute-done((f32[512,128]{1,0:T(8,128)S(1)}, f32[512,128]{1,0:T(8,128)S(1)}, u32[]{:S(2)}, u32[]{:S(2)}) %collective-permute-start.5) | collective-permute-done | bytes 262176 | tf_op jit(solution)/shard_map/ppermute | solution.py:255
  71.6 2.3 collective-permute-done.6
  74.5 3.0 %merge_state.1 = f32[32,8,16,128]{3,2,1,0:T(8,128)} custom-call(f32[32,16,128]{2,1,0:T(8,128)} %bitcast.34, f32[32,16,128]{2,1,0:T(8,128)} %bitcast.50, f32[32,16,128]{2,1,0:T(8,128)} %bitcast.51, f32[32,16,128]{2,1,0:T(8,128)} %bitcast.52, f32[32,16,128]{2,1,0:T(8,128)} %bitcast.53, f32[32,16,128]{2,1,0:T(8,128)} %bitcast.54, f32[32,16,128]{2,1,0:T(8,128)} %bitcast.55, ...), custom_call_target="tpu_custom_call" | custom-call | tf_op jit(solution)/shard_map/merge_state/pallas_call | solution.py:301
  77.5 8.6 %all-to-all-start = ((f32[32,8,16,128]{3,2,1,0:T(8,128)}), f32[32,8,16,128]{3,2,1,0:T(8,128)S(1)}, u32[]{:S(2)}, u32[]{:S(2)}) async-start(f32[32,8,16,128]{3,2,1,0:T(8,128)} %merge_state.1), calls=%async_computation | async-start | bytes 4194304 | tf_op jit(solution)/shard_map/all_to_all | solution.py:260
  86.1 3.0 %spread_adjoint.1 = (f32[32,16,128]{2,1,0:T(8,128)}, f32[32,16,128]{2,1,0:T(8,128)}, f32[32,16,128]{2,1,0:T(8,128)}, f32[32,16,128]{2,1,0:T(8,128)}, f32[32,16,1...) custom-call(f32[32,8,16,128]{3,2,1,0:T(8,128)} %all-to-all-done.1.in_ref), custom_call_target="tpu_custom_call" | custom-call | tf_op jit(solution)/shard_map/spread_adjoint/pallas_call | solution.py:292
  89.1 3.3 %collective-permute-start.7 = (f32[32,16,128]{2,1,0:T(8,128)}, f32[32,16,128]{2,1,0:T(8,128)S(1)}, u32[]{:S(2)}, u32[]{:S(2)}) collective-permute-start(f32[32,16,128]{2,1,0:T(8,128)} %get-tuple-element.48), channel_id=1, source_target_pairs={{0,8},{8,1},{1,9},{9,2},{2,10},{10,3},{3,11},{11,0},{4,12},{12,5},... | collective-permute-start | bytes 786440 | tf_op jit(solution)/shard_map/ppermute | solution.py:255
  92.4 0.8 collective-permute-start.8
  93.6 4.5 %collective-permute-start.10 = (f32[32,16,128]{2,1,0:T(8,128)}, f32[32,16,128]{2,1,0:T(8,128)S(1)}, u32[]{:S(2)}, u32[]{:S(2)}) collective-permute-start(f32[32,16,128]{2,1,0:T(8,128)} %get-tuple-element.51), channel_id=1, source_target_pairs={{0,2},{8,10},{1,3},{9,11},{2,0},{10,8},{3,1},{11,9},{4,6},{12,14},... | collective-permute-start | bytes 786440 | tf_op jit(solution)/shard_map/ppermute | solution.py:255
  98.1 1.1 collective-permute-start.11
  99.2 2.1 collective-permute-start.12
  101.3 9.9 %collective-permute-done.8 = f32[32,16,128]{2,1,0:T(8,128)S(1)} collective-permute-done((f32[32,16,128]{2,1,0:T(8,128)}, f32[32,16,128]{2,1,0:T(8,128)S(1)}, u32[]{:S(2)}, u32[]{:S(2)}) %collective-permute-start.8) | collective-permute-done | bytes 262176 | tf_op jit(solution)/shard_map/ppermute | solution.py:255
  111.1 3.3 %all-to-all-done = f32[32,8,16,128]{3,2,1,0:T(8,128)S(1)} async-done(((f32[32,8,16,128]{3,2,1,0:T(8,128)}), f32[32,8,16,128]{3,2,1,0:T(8,128)S(1)}, u32[]{:S(2)}, u32[]{:S(2)}) %all-to-all-start) | async-done | bytes 2097184 | tf_op jit(solution)/shard_map/all_to_all | solution.py:260
  114.4 1.0 copy-done.12
  115.4 1.0 copy-done.14
  116.5 1.0 copy-done.18
  117.5 1.0 copy-done.20
  118.6 1.0 copy-done.22
  119.6 1.0 copy-done.24
  120.7 4.7 %state.1.state_ref = f32[1024,512]{1,0:T(8,128)S(1)} custom-call(s32[1]{0:T(128)} %bitcast.z_ref.refs_0_, f32[32,8,2,8,128]{4,3,2,1,0:T(8,128)S(1)} %bitcast.33, bf16[512,512]{1,0:T(8,128)(2,1)S(1)} %copy-done.14, bf16[512,512]{1,0:T(8,128)(2,1)S(1)} %copy-done.12, bf16[512,512]{1,0:T(8,128)(2,1)S(1)} %copy-done.24, bf16[512,512]{1,0:T(8,128)(2,1)S(1)} %copy-done.22, ...), custom_call_target="tpu_custom_call" | custom-call | flops 3221225472 | bytes 7340032 | tf_op jit(solution)/shard_map/state/pallas_call | solution.py:223
  125.4 9.6 %collective-permute-done.10 = f32[32,16,128]{2,1,0:T(8,128)S(1)} collective-permute-done((f32[32,16,128]{2,1,0:T(8,128)}, f32[32,16,128]{2,1,0:T(8,128)S(1)}, u32[]{:S(2)}, u32[]{:S(2)}) %collective-permute-start.10) | collective-permute-done | bytes 262176 | tf_op jit(solution)/shard_map/ppermute | solution.py:255
  134.9 4.7 %collective-permute-done.12 = f32[32,16,128]{2,1,0:T(8,128)} collective-permute-done((f32[32,16,128]{2,1,0:T(8,128)}, f32[32,16,128]{2,1,0:T(8,128)}, u32[]{:S(2)}, u32[]{:S(2)}) %collective-permute-start.12) | collective-permute-done | bytes 262176 | tf_op jit(solution)/shard_map/ppermute | solution.py:255
  139.6 5.6 %collective-permute-done.13 = f32[32,16,128]{2,1,0:T(8,128)} collective-permute-done((f32[32,16,128]{2,1,0:T(8,128)}, f32[32,16,128]{2,1,0:T(8,128)}, u32[]{:S(2)}, u32[]{:S(2)}) %collective-permute-start.13) | collective-permute-done | bytes 262176 | tf_op jit(solution)/shard_map/ppermute | solution.py:255
  145.3 8.4 %grid.1 = (f32[32,8,128]{2,1,0:T(8,128)S(1)}, f32[32,8,128]{2,1,0:T(8,128)S(1)}, f32[32,8,128]{2,1,0:T(8,128)S(1)}, f32[32,8,128]{2,1,0:T(8,128)S(1)}, f32[32,8,...) custom-call(s32[1]{0:T(128)} %bitcast.z_ref.refs_0_, ...), custom_call_target="tpu_custom_call" | custom-call | flops 4831838208 | bytes 9437184 | tf_op jit(solution)/shard_map/grid/pallas_call | solution.py:223
  154.4 3.4 %odd.1 = f32[32,8,8,128]{3,2,1,0:T(8,128)} custom-call(s32[1]{0:T(128)} %bitcast.z_ref.refs_0_, bf16[512,512]{1,0:T(8,128)(2,1)S(1)} %get-tuple-element.55.odd_h_ref, bf16[512,512]{1,0:T(8,128)(2,1)S(1)} %get-tuple-element.56.odd_l_ref, bf16[512,512]{1,0:T(8,128)(2,1)S(1)} %copy-done.15, bf16[512,512]{1,0:T(8,128)(2,1)S(1)} %copy-done.13, ...), custom_call_target="tpu_custom_call" | custom-call | flops 1610612736 | bytes 4194304 | tf_op jit(solution)/shard_map/odd/pallas_call | solution.py:223
  157.7 7.7 %all-to-all-start.2 = ((f32[32,8,8,128]{3,2,1,0:T(8,128)}), f32[32,8,8,128]{3,2,1,0:T(8,128)S(1)}, u32[]{:S(2)}, u32[]{:S(2)}) async-start(f32[32,8,8,128]{3,2,1,0:T(8,128)} %odd.1), calls=%async_computation.2 | async-start | bytes 2097152 | tf_op jit(solution)/shard_map/all_to_all | solution.py:260
  165.7 1.5 collective-permute-start.22
  167.3 3.4 %collective-permute-start.23 = (f32[32,8,128]{2,1,0:T(8,128)S(1)}, f32[32,8,128]{2,1,0:T(8,128)S(1)}, u32[]{:S(2)}, u32[]{:S(2)}) collective-permute-start(f32[32,8,128]{2,1,0:T(8,128)S(1)} %get-tuple-element.68), channel_id=1, source_target_pairs={{0,9},{8,2},{1,10},{9,3},{2,11},{10,0},{3,8},{11,1},{4,13},{12,6},... | collective-permute-start | bytes 393224 | tf_op jit(solution)/shard_map/ppermute | solution.py:255
  170.6 0.8 collective-permute-start.24
  171.4 4.2 %collective-permute-start.25 = (f32[32,8,128]{2,1,0:T(8,128)S(1)}, f32[32,8,128]{2,1,0:T(8,128)S(1)}, u32[]{:S(2)}, u32[]{:S(2)}) collective-permute-start(f32[32,8,128]{2,1,0:T(8,128)S(1)} %get-tuple-element.70), channel_id=1, source_target_pairs={{0,10},{8,3},{1,11},{9,0},{2,8},{10,1},{3,9},{11,2},{4,14},{12,7},... | collective-permute-start | bytes 393224 | tf_op jit(solution)/shard_map/ppermute | solution.py:255
  175.6 2.7 %collective-permute-start.26 = (f32[32,8,128]{2,1,0:T(8,128)S(1)}, f32[32,8,128]{2,1,0:T(8,128)S(1)}, u32[]{:S(2)}, u32[]{:S(2)}) collective-permute-start(f32[32,8,128]{2,1,0:T(8,128)S(1)} %get-tuple-element.71), channel_id=1, source_target_pairs={{0,3},{8,11},{1,0},{9,8},{2,1},{10,9},{3,2},{11,10},{4,7},{12,15},... | collective-permute-start | bytes 393224 | tf_op jit(solution)/shard_map/ppermute | solution.py:255
  178.3 9.1 %collective-permute-done.23.refs_3_ = f32[32,8,128]{2,1,0:T(8,128)S(1)} collective-permute-done((f32[32,8,128]{2,1,0:T(8,128)S(1)}, f32[32,8,128]{2,1,0:T(8,128)S(1)}, u32[]{:S(2)}, u32[]{:S(2)}) %collective-permute-start.23) | collective-permute-done | bytes 131104 | tf_op jit(solution)/shard_map/ppermute | solution.py:255
  187.4 4.1 %collective-permute-done.24.refs_4_ = f32[32,8,128]{2,1,0:T(8,128)S(1)} collective-permute-done((f32[32,8,128]{2,1,0:T(8,128)S(1)}, f32[32,8,128]{2,1,0:T(8,128)S(1)}, u32[]{:S(2)}, u32[]{:S(2)}) %collective-permute-start.24) | collective-permute-done | bytes 131104 | tf_op jit(solution)/shard_map/ppermute | solution.py:255
  191.5 4.6 %collective-permute-done.26.refs_6_ = f32[32,8,128]{2,1,0:T(8,128)S(1)} collective-permute-done((f32[32,8,128]{2,1,0:T(8,128)S(1)}, f32[32,8,128]{2,1,0:T(8,128)S(1)}, u32[]{:S(2)}, u32[]{:S(2)}) %collective-permute-start.26) | collective-permute-done | bytes 131104 | tf_op jit(solution)/shard_map/ppermute | solution.py:255
  197.3 2.4 merge_even.1
  199.8 7.8 %all-to-all-start.3 = ((f32[32,8,8,128]{3,2,1,0:T(8,128)}), f32[32,8,8,128]{3,2,1,0:T(8,128)S(1)}, u32[]{:S(2)}, u32[]{:S(2)}) async-start(f32[32,8,8,128]{3,2,1,0:T(8,128)} %merge_even.1), calls=%async_computation.3 | async-start | bytes 2097152 | tf_op jit(solution)/shard_map/all_to_all | solution.py:260
  207.5 2.2 spread_odd.1
  209.8 3.0 %collective-permute-start.14 = (f32[32,8,128]{2,1,0:T(8,128)}, f32[32,8,128]{2,1,0:T(8,128)S(1)}, u32[]{:S(2)}, u32[]{:S(2)}) collective-permute-start(f32[32,8,128]{2,1,0:T(8,128)} %get-tuple-element.58), channel_id=1, source_target_pairs={{0,8},{8,1},{1,9},{9,2},{2,10},{10,3},{3,11},{11,0},{4,12},{12,5},... | collective-permute-start | bytes 393224 | tf_op jit(solution)/shard_map/ppermute | solution.py:255
  212.7 0.9 collective-permute-start.15
  214.0 4.5 %collective-permute-start.17 = (f32[32,8,128]{2,1,0:T(8,128)}, f32[32,8,128]{2,1,0:T(8,128)S(1)}, u32[]{:S(2)}, u32[]{:S(2)}) collective-permute-start(f32[32,8,128]{2,1,0:T(8,128)} %get-tuple-element.61), channel_id=1, source_target_pairs={{0,2},{8,10},{1,3},{9,11},{2,0},{10,8},{3,1},{11,9},{4,6},{12,14},... | collective-permute-start | bytes 393224 | tf_op jit(solution)/shard_map/ppermute | solution.py:255
  218.5 1.4 collective-permute-start.18
  219.9 1.8 collective-permute-start.19
  221.7 2.2 collective-permute-done.15
  224.5 2.4 radial_even.1.refs_11_
  226.8 2.2 collective-permute-done.16
  229.1 5.5 %collective-permute-done.17 = f32[32,8,128]{2,1,0:T(8,128)S(1)} collective-permute-done((f32[32,8,128]{2,1,0:T(8,128)}, f32[32,8,128]{2,1,0:T(8,128)S(1)}, u32[]{:S(2)}, u32[]{:S(2)}) %collective-permute-start.17) | collective-permute-done | bytes 131104 | tf_op jit(solution)/shard_map/ppermute | solution.py:255
  234.5 5.9 %collective-permute-done.19 = f32[32,8,128]{2,1,0:T(8,128)S(1)} collective-permute-done((f32[32,8,128]{2,1,0:T(8,128)}, f32[32,8,128]{2,1,0:T(8,128)S(1)}, u32[]{:S(2)}, u32[]{:S(2)}) %collective-permute-start.19) | collective-permute-done | bytes 131104 | tf_op jit(solution)/shard_map/ppermute | solution.py:255
  240.4 2.7 %collective-permute-done.20 = f32[32,8,128]{2,1,0:T(8,128)S(1)} collective-permute-done((f32[32,8,128]{2,1,0:T(8,128)}, f32[32,8,128]{2,1,0:T(8,128)S(1)}, u32[]{:S(2)}, u32[]{:S(2)}) %collective-permute-start.20) | collective-permute-done | bytes 131104 | tf_op jit(solution)/shard_map/ppermute | solution.py:255
  243.1 1.8 radial_odd.1
  (93 shorter events, 4.6 us)
Async XLA Ops:
  0.0 1.6 copy-start
  7.1 8.9 %copy-start.5 = (bf16[512,256]{1,0:T(8,128)(2,1)S(1)}, bf16[512,256]{1,0:T(8,128)(2,1)}, u32[]{:S(2)}) copy-start(bf16[512,256]{1,0:T(8,128)(2,1)} %constant.36.clone.tl_ref) | copy-start | bytes 786436
  7.1 8.9 %copy-start.7 = (bf16[512,256]{1,0:T(8,128)(2,1)S(1)}, bf16[512,256]{1,0:T(8,128)(2,1)}, u32[]{:S(2)}) copy-start(bf16[512,256]{1,0:T(8,128)(2,1)} %constant.35.clone.th_ref) | copy-start | bytes 786436
  7.1 8.9 %copy-start.10 = (f32[16,256,128]{2,1,0:T(8,128)S(1)}, f32[16,256,128]{2,1,0:T(8,128)}, u32[]{:S(2)}) copy-start(f32[16,256,128]{2,1,0:T(8,128)} %param.14) | copy-start | bytes 6291460
  7.1 70.4 %all-to-all-start.1 = ((f32[32,8,16,128]{3,2,1,0:T(8,128)}), f32[32,8,16,128]{3,2,1,0:T(8,128)}, u32[]{:S(2)}, u32[]{:S(2)}) async-start(f32[32,8,16,128]{3,2,1,0:T(8,128)} %bitcast.12), calls=%async_computation.1 | async-start | bytes 4194304 | tf_op jit(solution)/shard_map/all_to_all | solution.py:260
  18.5 13.3 %collective-permute-start = (f32[512,128]{1,0:T(8,128)S(1)}, f32[512,128]{1,0:T(8,128)S(1)}, u32[]{:S(2)}, u32[]{:S(2)}) collective-permute-start(f32[512,128]{1,0:T(8,128)S(1)} %get-tuple-element.40), channel_id=1, source_target_pairs={{0,8},{8,1},{1,9},{9,2},{2,10},{10,3},{3,11},{11,0},{4,12},{12,5},... | collective-permute-start | bytes 786440 | tf_op jit(solution)/shard_map/ppermute | solution.py:255
  20.1 17.6 %collective-permute-start.1 = (f32[512,128]{1,0:T(8,128)S(1)}, f32[512,128]{1,0:T(8,128)S(1)}, u32[]{:S(2)}, u32[]{:S(2)}) collective-permute-start(f32[512,128]{1,0:T(8,128)S(1)} %get-tuple-element.41), channel_id=1, source_target_pairs={{0,1},{8,9},{1,2},{9,10},{2,3},{10,11},{3,0},{11,8},{4,5},{12,13},... | collective-permute-start | bytes 786440 | tf_op jit(solution)/shard_map/ppermute | solution.py:255
  23.1 36.0 %collective-permute-start.2 = (f32[512,128]{1,0:T(8,128)S(1)}, f32[512,128]{1,0:T(8,128)S(1)}, u32[]{:S(2)}, u32[]{:S(2)}) collective-permute-start(f32[512,128]{1,0:T(8,128)S(1)} %get-tuple-element.42), channel_id=1, source_target_pairs={{0,9},{8,2},{1,10},{9,3},{2,11},{10,0},{3,8},{11,1},{4,13},{12,6},... | collective-permute-start | bytes 786440 | tf_op jit(solution)/shard_map/ppermute | solution.py:255
  26.8 37.0 %collective-permute-start.3 = (f32[512,128]{1,0:T(8,128)S(1)}, f32[512,128]{1,0:T(8,128)S(1)}, u32[]{:S(2)}, u32[]{:S(2)}) collective-permute-start(f32[512,128]{1,0:T(8,128)S(1)} %get-tuple-element.43), channel_id=1, source_target_pairs={{0,2},{8,10},{1,3},{9,11},{2,0},{10,8},{3,1},{11,9},{4,6},{12,14},... | collective-permute-start | bytes 786440 | tf_op jit(solution)/shard_map/ppermute | solution.py:255
  27.3 36.6 %collective-permute-start.4 = (f32[512,128]{1,0:T(8,128)S(1)}, f32[512,128]{1,0:T(8,128)S(1)}, u32[]{:S(2)}, u32[]{:S(2)}) collective-permute-start(f32[512,128]{1,0:T(8,128)S(1)} %get-tuple-element.44), channel_id=1, source_target_pairs={{0,10},{8,3},{1,11},{9,0},{2,8},{10,1},{3,9},{11,2},{4,14},{12,7},... | collective-permute-start | bytes 786440 | tf_op jit(solution)/shard_map/ppermute | solution.py:255
  31.8 42.1 %copy-start.27 = (f32[512,128]{1,0:T(8,128)}, f32[512,128]{1,0:T(8,128)S(1)}, u32[]{:S(2)}) copy-start(f32[512,128]{1,0:T(8,128)S(1)} %collective-permute-done) | copy-start | bytes 786436
  31.8 39.8 %collective-permute-start.5 = (f32[512,128]{1,0:T(8,128)S(1)}, f32[512,128]{1,0:T(8,128)S(1)}, u32[]{:S(2)}, u32[]{:S(2)}) collective-permute-start(f32[512,128]{1,0:T(8,128)S(1)} %get-tuple-element.45), channel_id=1, source_target_pairs={{0,3},{8,11},{1,0},{9,8},{2,1},{10,9},{3,2},{11,10},{4,7},{12,15},... | collective-permute-start | bytes 786440 | tf_op jit(solution)/shard_map/ppermute | solution.py:255
  37.7 36.1 %copy-start.28 = (f32[512,128]{1,0:T(8,128)}, f32[512,128]{1,0:T(8,128)S(1)}, u32[]{:S(2)}) copy-start(f32[512,128]{1,0:T(8,128)S(1)} %collective-permute-done.1) | copy-start | bytes 786436
  37.7 36.1 %collective-permute-start.6 = (f32[512,128]{1,0:T(8,128)S(1)}, f32[512,128]{1,0:T(8,128)S(1)}, u32[]{:S(2)}, u32[]{:S(2)}) collective-permute-start(f32[512,128]{1,0:T(8,128)S(1)} %get-tuple-element.46), channel_id=1, source_target_pairs={{0,11},{8,0},{1,8},{9,1},{2,9},{10,2},{3,10},{11,3},{4,15},{12,4},... | collective-permute-start | bytes 786440 | tf_op jit(solution)/shard_map/ppermute | solution.py:255
  59.0 14.8 %copy-start.29 = (f32[512,128]{1,0:T(8,128)}, f32[512,128]{1,0:T(8,128)S(1)}, u32[]{:S(2)}) copy-start(f32[512,128]{1,0:T(8,128)S(1)} %collective-permute-done.2) | copy-start | bytes 786436
  63.9 10.0 %copy-start.30 = (f32[512,128]{1,0:T(8,128)}, f32[512,128]{1,0:T(8,128)S(1)}, u32[]{:S(2)}) copy-start(f32[512,128]{1,0:T(8,128)S(1)} %collective-permute-done.3) | copy-start | bytes 786436
  63.9 10.0 %copy-start.31 = (f32[512,128]{1,0:T(8,128)}, f32[512,128]{1,0:T(8,128)S(1)}, u32[]{:S(2)}) copy-start(f32[512,128]{1,0:T(8,128)S(1)} %collective-permute-done.4) | copy-start | bytes 786436
  71.6 2.3 copy-start.32
  77.5 36.9 %all-to-all-start = ((f32[32,8,16,128]{3,2,1,0:T(8,128)}), f32[32,8,16,128]{3,2,1,0:T(8,128)S(1)}, u32[]{:S(2)}, u32[]{:S(2)}) async-start(f32[32,8,16,128]{3,2,1,0:T(8,128)} %merge_state.1), calls=%async_computation | async-start | bytes 4194304 | tf_op jit(solution)/shard_map/all_to_all | solution.py:260
  89.1 10.1 %collective-permute-start.7 = (f32[32,16,128]{2,1,0:T(8,128)}, f32[32,16,128]{2,1,0:T(8,128)S(1)}, u32[]{:S(2)}, u32[]{:S(2)}) collective-permute-start(f32[32,16,128]{2,1,0:T(8,128)} %get-tuple-element.48), channel_id=1, source_target_pairs={{0,8},{8,1},{1,9},{9,2},{2,10},{10,3},{3,11},{11,0},{4,12},{12,5},... | collective-permute-start | bytes 786440 | tf_op jit(solution)/shard_map/ppermute | solution.py:255
  92.4 18.7 %collective-permute-start.8 = (f32[32,16,128]{2,1,0:T(8,128)}, f32[32,16,128]{2,1,0:T(8,128)S(1)}, u32[]{:S(2)}, u32[]{:S(2)}) collective-permute-start(f32[32,16,128]{2,1,0:T(8,128)} %get-tuple-element.49), channel_id=1, source_target_pairs={{0,1},{8,9},{1,2},{9,10},{2,3},{10,11},{3,0},{11,8},{4,5},{12,13},... | collective-permute-start | bytes 786440 | tf_op jit(solution)/shard_map/ppermute | solution.py:255
  93.2 32.1 %collective-permute-start.9 = (f32[32,16,128]{2,1,0:T(8,128)}, f32[32,16,128]{2,1,0:T(8,128)S(1)}, u32[]{:S(2)}, u32[]{:S(2)}) collective-permute-start(f32[32,16,128]{2,1,0:T(8,128)} %get-tuple-element.50), channel_id=1, source_target_pairs={{0,9},{8,2},{1,10},{9,3},{2,11},{10,0},{3,8},{11,1},{4,13},{12,6},... | collective-permute-start | bytes 786440 | tf_op jit(solution)/shard_map/ppermute | solution.py:255
  93.6 41.4 %collective-permute-start.10 = (f32[32,16,128]{2,1,0:T(8,128)}, f32[32,16,128]{2,1,0:T(8,128)S(1)}, u32[]{:S(2)}, u32[]{:S(2)}) collective-permute-start(f32[32,16,128]{2,1,0:T(8,128)} %get-tuple-element.51), channel_id=1, source_target_pairs={{0,2},{8,10},{1,3},{9,11},{2,0},{10,8},{3,1},{11,9},{4,6},{12,14},... | collective-permute-start | bytes 786440 | tf_op jit(solution)/shard_map/ppermute | solution.py:255
  98.1 36.9 %collective-permute-start.11 = (f32[32,16,128]{2,1,0:T(8,128)}, f32[32,16,128]{2,1,0:T(8,128)S(1)}, u32[]{:S(2)}, u32[]{:S(2)}) collective-permute-start(f32[32,16,128]{2,1,0:T(8,128)} %get-tuple-element.52), channel_id=1, source_target_pairs={{0,10},{8,3},{1,11},{9,0},{2,8},{10,1},{3,9},{11,2},{4,14},{12,7},... | collective-permute-start | bytes 786440 | tf_op jit(solution)/shard_map/ppermute | solution.py:255
  99.2 40.4 %collective-permute-start.12 = (f32[32,16,128]{2,1,0:T(8,128)}, f32[32,16,128]{2,1,0:T(8,128)}, u32[]{:S(2)}, u32[]{:S(2)}) collective-permute-start(f32[32,16,128]{2,1,0:T(8,128)} %get-tuple-element.53), channel_id=1, source_target_pairs={{0,3},{8,11},{1,0},{9,8},{2,1},{10,9},{3,2},{11,10},{4,7},{12,15},... | collective-permute-start | bytes 786440 | tf_op jit(solution)/shard_map/ppermute | solution.py:255
  111.1 34.0 %collective-permute-start.13 = (f32[32,16,128]{2,1,0:T(8,128)}, f32[32,16,128]{2,1,0:T(8,128)}, u32[]{:S(2)}, u32[]{:S(2)}) collective-permute-start(f32[32,16,128]{2,1,0:T(8,128)} %get-tuple-element.54), channel_id=1, source_target_pairs={{0,11},{8,0},{1,8},{9,1},{2,9},{10,2},{3,10},{11,3},{4,15},{12,4},... | collective-permute-start | bytes 786440 | tf_op jit(solution)/shard_map/ppermute | solution.py:255
  114.4 1.0 copy-start.12
  115.4 1.0 copy-start.14
  116.5 1.0 copy-start.18
  117.5 1.0 copy-start.20
  120.7 24.5 %copy-start.11 = (f32[32,16,128]{2,1,0:T(8,128)S(1)}, f32[32,16,128]{2,1,0:T(8,128)}, u32[]{:S(2)}) copy-start(f32[32,16,128]{2,1,0:T(8,128)} %get-tuple-element.47) | copy-start | bytes 786436
  120.7 24.5 %copy-start.13 = (bf16[512,512]{1,0:T(8,128)(2,1)S(1)}, bf16[512,512]{1,0:T(8,128)(2,1)}, u32[]{:S(2)}) copy-start(bf16[512,512]{1,0:T(8,128)(2,1)} %constant.38.clone.yl_ref) | copy-start | bytes 1572868
  120.7 24.5 %copy-start.15 = (bf16[512,512]{1,0:T(8,128)(2,1)S(1)}, bf16[512,512]{1,0:T(8,128)(2,1)}, u32[]{:S(2)}) copy-start(bf16[512,512]{1,0:T(8,128)(2,1)} %constant.37.clone.yh_ref) | copy-start | bytes 1572868
  120.7 24.5 %copy-start.19 = (bf16[512,512]{1,0:T(8,128)(2,1)S(1)}, bf16[512,512]{1,0:T(8,128)(2,1)}, u32[]{:S(2)}) copy-start(bf16[512,512]{1,0:T(8,128)(2,1)} %constant.42.clone.ol_ref) | copy-start | bytes 1572868
  120.7 24.6 %copy-start.21 = (bf16[512,512]{1,0:T(8,128)(2,1)S(1)}, bf16[512,512]{1,0:T(8,128)(2,1)}, u32[]{:S(2)}) copy-start(bf16[512,512]{1,0:T(8,128)(2,1)} %constant.41.clone.oh_ref) | copy-start | bytes 1572868
  120.7 24.6 %copy-start.23 = (bf16[512,512]{1,0:T(8,128)(2,1)S(1)}, bf16[512,512]{1,0:T(8,128)(2,1)}, u32[]{:S(2)}) copy-start(bf16[512,512]{1,0:T(8,128)(2,1)} %constant.40.clone.el_ref) | copy-start | bytes 1572868
  120.7 24.5 %copy-start.25 = (bf16[512,512]{1,0:T(8,128)(2,1)S(1)}, bf16[512,512]{1,0:T(8,128)(2,1)}, u32[]{:S(2)}) copy-start(bf16[512,512]{1,0:T(8,128)(2,1)} %constant.39.clone.eh_ref) | copy-start | bytes 1572868
  145.2 9.1 %copy-start.16 = (bf16[512,512]{1,0:T(8,128)(2,1)S(1)}, bf16[512,512]{1,0:T(8,128)(2,1)}, u32[]{:S(2)}) copy-start(bf16[512,512]{1,0:T(8,128)(2,1)} %constant.44.clone.pl_ref) | copy-start | bytes 1572868
  145.3 9.1 %copy-start.17 = (bf16[512,512]{1,0:T(8,128)(2,1)S(1)}, bf16[512,512]{1,0:T(8,128)(2,1)}, u32[]{:S(2)}) copy-start(bf16[512,512]{1,0:T(8,128)(2,1)} %constant.43.clone.ph_ref) | copy-start | bytes 1572868
  157.7 42.0 %all-to-all-start.2 = ((f32[32,8,8,128]{3,2,1,0:T(8,128)}), f32[32,8,8,128]{3,2,1,0:T(8,128)S(1)}, u32[]{:S(2)}, u32[]{:S(2)}) async-start(f32[32,8,8,128]{3,2,1,0:T(8,128)} %odd.1), calls=%async_computation.2 | async-start | bytes 2097152 | tf_op jit(solution)/shard_map/all_to_all | solution.py:260
  165.4 10.2 %collective-permute-start.21 = (f32[32,8,128]{2,1,0:T(8,128)S(1)}, f32[32,8,128]{2,1,0:T(8,128)S(1)}, u32[]{:S(2)}, u32[]{:S(2)}) collective-permute-start(f32[32,8,128]{2,1,0:T(8,128)S(1)} %get-tuple-element.66), channel_id=1, source_target_pairs={{0,8},{8,1},{1,9},{9,2},{2,10},{10,3},{3,11},{11,0},{4,12},{12,5},... | collective-permute-start | bytes 393224 | tf_op jit(solution)/shard_map/ppermute | solution.py:255
  165.7 12.6 %collective-permute-start.22 = (f32[32,8,128]{2,1,0:T(8,128)S(1)}, f32[32,8,128]{2,1,0:T(8,128)S(1)}, u32[]{:S(2)}, u32[]{:S(2)}) collective-permute-start(f32[32,8,128]{2,1,0:T(8,128)S(1)} %get-tuple-element.67), channel_id=1, source_target_pairs={{0,1},{8,9},{1,2},{9,10},{2,3},{10,11},{3,0},{11,8},{4,5},{12,13},... | collective-permute-start | bytes 393224 | tf_op jit(solution)/shard_map/ppermute | solution.py:255
  167.3 20.1 %collective-permute-start.23 = (f32[32,8,128]{2,1,0:T(8,128)S(1)}, f32[32,8,128]{2,1,0:T(8,128)S(1)}, u32[]{:S(2)}, u32[]{:S(2)}) collective-permute-start(f32[32,8,128]{2,1,0:T(8,128)S(1)} %get-tuple-element.68), channel_id=1, source_target_pairs={{0,9},{8,2},{1,10},{9,3},{2,11},{10,0},{3,8},{11,1},{4,13},{12,6},... | collective-permute-start | bytes 393224 | tf_op jit(solution)/shard_map/ppermute | solution.py:255
  170.6 20.8 %collective-permute-start.24 = (f32[32,8,128]{2,1,0:T(8,128)S(1)}, f32[32,8,128]{2,1,0:T(8,128)S(1)}, u32[]{:S(2)}, u32[]{:S(2)}) collective-permute-start(f32[32,8,128]{2,1,0:T(8,128)S(1)} %get-tuple-element.69), channel_id=1, source_target_pairs={{0,2},{8,10},{1,3},{9,11},{2,0},{10,8},{3,1},{11,9},{4,6},{12,14},... | collective-permute-start | bytes 393224 | tf_op jit(solution)/shard_map/ppermute | solution.py:255
  171.4 20.1 %collective-permute-start.25 = (f32[32,8,128]{2,1,0:T(8,128)S(1)}, f32[32,8,128]{2,1,0:T(8,128)S(1)}, u32[]{:S(2)}, u32[]{:S(2)}) collective-permute-start(f32[32,8,128]{2,1,0:T(8,128)S(1)} %get-tuple-element.70), channel_id=1, source_target_pairs={{0,10},{8,3},{1,11},{9,0},{2,8},{10,1},{3,9},{11,2},{4,14},{12,7},... | collective-permute-start | bytes 393224 | tf_op jit(solution)/shard_map/ppermute | solution.py:255
  175.6 21.1 %copy-start.34 = (f32[32,8,128]{2,1,0:T(8,128)}, f32[32,8,128]{2,1,0:T(8,128)S(1)}, u32[]{:S(2)}) copy-start(f32[32,8,128]{2,1,0:T(8,128)S(1)} %collective-permute-done.21.refs_1_) | copy-start | bytes 393220
  175.6 20.5 %collective-permute-start.26 = (f32[32,8,128]{2,1,0:T(8,128)S(1)}, f32[32,8,128]{2,1,0:T(8,128)S(1)}, u32[]{:S(2)}, u32[]{:S(2)}) collective-permute-start(f32[32,8,128]{2,1,0:T(8,128)S(1)} %get-tuple-element.71), channel_id=1, source_target_pairs={{0,3},{8,11},{1,0},{9,8},{2,1},{10,9},{3,2},{11,10},{4,7},{12,15},... | collective-permute-start | bytes 393224 | tf_op jit(solution)/shard_map/ppermute | solution.py:255
  178.3 18.4 %copy-start.35 = (f32[32,8,128]{2,1,0:T(8,128)}, f32[32,8,128]{2,1,0:T(8,128)S(1)}, u32[]{:S(2)}) copy-start(f32[32,8,128]{2,1,0:T(8,128)S(1)} %collective-permute-done.22.refs_2_) | copy-start | bytes 393220
  178.3 18.4 %collective-permute-start.27 = (f32[32,8,128]{2,1,0:T(8,128)S(1)}, f32[32,8,128]{2,1,0:T(8,128)S(1)}, u32[]{:S(2)}, u32[]{:S(2)}) collective-permute-start(f32[32,8,128]{2,1,0:T(8,128)S(1)} %get-tuple-element.72), channel_id=1, source_target_pairs={{0,11},{8,0},{1,8},{9,1},{2,9},{10,2},{3,10},{11,3},{4,15},{12,4},... | collective-permute-start | bytes 393224 | tf_op jit(solution)/shard_map/ppermute | solution.py:255
  187.4 9.3 %copy-start.36 = (f32[32,8,128]{2,1,0:T(8,128)}, f32[32,8,128]{2,1,0:T(8,128)S(1)}, u32[]{:S(2)}) copy-start(f32[32,8,128]{2,1,0:T(8,128)S(1)} %collective-permute-done.23.refs_3_) | copy-start | bytes 393220
  191.5 5.2 %copy-start.37 = (f32[32,8,128]{2,1,0:T(8,128)}, f32[32,8,128]{2,1,0:T(8,128)S(1)}, u32[]{:S(2)}) copy-start(f32[32,8,128]{2,1,0:T(8,128)S(1)} %collective-permute-done.24.refs_4_) | copy-start | bytes 393220
  191.5 5.2 %copy-start.38 = (f32[32,8,128]{2,1,0:T(8,128)}, f32[32,8,128]{2,1,0:T(8,128)S(1)}, u32[]{:S(2)}) copy-start(f32[32,8,128]{2,1,0:T(8,128)S(1)} %collective-permute-done.25.refs_5_) | copy-start | bytes 393220
  199.7 24.7 %copy-start.1 = (bf16[256,256]{1,0:T(8,128)(2,1)S(1)}, bf16[256,256]{1,0:T(8,128)(2,1)}, u32[]{:S(2)}) copy-start(bf16[256,256]{1,0:T(8,128)(2,1)} %constant.46.clone.tl_ref.refs_2_) | copy-start | bytes 393220
  199.7 24.7 %copy-start.2 = (bf16[256,256]{1,0:T(8,128)(2,1)S(1)}, bf16[256,256]{1,0:T(8,128)(2,1)}, u32[]{:S(2)}) copy-start(bf16[256,256]{1,0:T(8,128)(2,1)} %constant.45.clone.th_ref.refs_1_) | copy-start | bytes 393220
  199.8 7.8 %copy-start.26 = (f32[32,8,8,128]{3,2,1,0:T(8,128)}, f32[32,8,8,128]{3,2,1,0:T(8,128)S(1)}, u32[]{:S(2)}) copy-start(f32[32,8,8,128]{3,2,1,0:T(8,128)S(1)} %all-to-all-done.2.in_ref) | copy-start | bytes 3145732
  199.8 24.7 %all-to-all-start.3 = ((f32[32,8,8,128]{3,2,1,0:T(8,128)}), f32[32,8,8,128]{3,2,1,0:T(8,128)S(1)}, u32[]{:S(2)}, u32[]{:S(2)}) async-start(f32[32,8,8,128]{3,2,1,0:T(8,128)} %merge_even.1), calls=%async_computation.3 | async-start | bytes 2097152 | tf_op jit(solution)/shard_map/all_to_all | solution.py:260
  209.8 33.3 %copy-start.9 = (f32[32,8,128]{2,1,0:T(8,128)S(1)}, f32[32,8,128]{2,1,0:T(8,128)}, u32[]{:S(2)}) copy-start(f32[32,8,128]{2,1,0:T(8,128)} %get-tuple-element.57) | copy-start | bytes 393220
  209.8 10.1 %collective-permute-start.14 = (f32[32,8,128]{2,1,0:T(8,128)}, f32[32,8,128]{2,1,0:T(8,128)S(1)}, u32[]{:S(2)}, u32[]{:S(2)}) collective-permute-start(f32[32,8,128]{2,1,0:T(8,128)} %get-tuple-element.58), channel_id=1, source_target_pairs={{0,8},{8,1},{1,9},{9,2},{2,10},{10,3},{3,11},{11,0},{4,12},{12,5},... | collective-permute-start | bytes 393224 | tf_op jit(solution)/shard_map/ppermute | solution.py:255
  212.7 11.2 %collective-permute-start.15 = (f32[32,8,128]{2,1,0:T(8,128)}, f32[32,8,128]{2,1,0:T(8,128)S(1)}, u32[]{:S(2)}, u32[]{:S(2)}) collective-permute-start(f32[32,8,128]{2,1,0:T(8,128)} %get-tuple-element.59), channel_id=1, source_target_pairs={{0,1},{8,9},{1,2},{9,10},{2,3},{10,11},{3,0},{11,8},{4,5},{12,13},... | collective-permute-start | bytes 393224 | tf_op jit(solution)/shard_map/ppermute | solution.py:255
  213.6 15.4 %collective-permute-start.16 = (f32[32,8,128]{2,1,0:T(8,128)}, f32[32,8,128]{2,1,0:T(8,128)S(1)}, u32[]{:S(2)}, u32[]{:S(2)}) collective-permute-start(f32[32,8,128]{2,1,0:T(8,128)} %get-tuple-element.60), channel_id=1, source_target_pairs={{0,9},{8,2},{1,10},{9,3},{2,11},{10,0},{3,8},{11,1},{4,13},{12,6},... | collective-permute-start | bytes 393224 | tf_op jit(solution)/shard_map/ppermute | solution.py:255
  214.0 20.5 %collective-permute-start.17 = (f32[32,8,128]{2,1,0:T(8,128)}, f32[32,8,128]{2,1,0:T(8,128)S(1)}, u32[]{:S(2)}, u32[]{:S(2)}) collective-permute-start(f32[32,8,128]{2,1,0:T(8,128)} %get-tuple-element.61), channel_id=1, source_target_pairs={{0,2},{8,10},{1,3},{9,11},{2,0},{10,8},{3,1},{11,9},{4,6},{12,14},... | collective-permute-start | bytes 393224 | tf_op jit(solution)/shard_map/ppermute | solution.py:255
  218.5 16.1 %collective-permute-start.18 = (f32[32,8,128]{2,1,0:T(8,128)}, f32[32,8,128]{2,1,0:T(8,128)S(1)}, u32[]{:S(2)}, u32[]{:S(2)}) collective-permute-start(f32[32,8,128]{2,1,0:T(8,128)} %get-tuple-element.62), channel_id=1, source_target_pairs={{0,10},{8,3},{1,11},{9,0},{2,8},{10,1},{3,9},{11,2},{4,14},{12,7},... | collective-permute-start | bytes 393224 | tf_op jit(solution)/shard_map/ppermute | solution.py:255
  219.9 20.5 %collective-permute-start.19 = (f32[32,8,128]{2,1,0:T(8,128)}, f32[32,8,128]{2,1,0:T(8,128)S(1)}, u32[]{:S(2)}, u32[]{:S(2)}) collective-permute-start(f32[32,8,128]{2,1,0:T(8,128)} %get-tuple-element.63), channel_id=1, source_target_pairs={{0,3},{8,11},{1,0},{9,8},{2,1},{10,9},{3,2},{11,10},{4,7},{12,15},... | collective-permute-start | bytes 393224 | tf_op jit(solution)/shard_map/ppermute | solution.py:255
  224.0 19.1 %collective-permute-start.20 = (f32[32,8,128]{2,1,0:T(8,128)}, f32[32,8,128]{2,1,0:T(8,128)S(1)}, u32[]{:S(2)}, u32[]{:S(2)}) collective-permute-start(f32[32,8,128]{2,1,0:T(8,128)} %get-tuple-element.64), channel_id=1, source_target_pairs={{0,11},{8,0},{1,8},{9,1},{2,9},{10,2},{3,10},{11,3},{4,15},{12,4},... | collective-permute-start | bytes 393224 | tf_op jit(solution)/shard_map/ppermute | solution.py:255
  (9 other events, 7.3 us)

commit v3 on v1

v3 whole, which is shorter than its diff:
```python
import functools
import math

import jax
import jax.numpy as jnp
import ml_dtypes
import numpy as np
from jax import lax
from jax.experimental import pallas as pl
from jax.experimental.pallas import tpu as pltpu
from jax.sharding import PartitionSpec as P

NX = 1024
NY = 512
NR = 256
BOTH = ("ax", "az")


def halves(table):
    high = table.astype(ml_dtypes.bfloat16)
    low = (table - high.astype(np.float64)).astype(ml_dtypes.bfloat16)
    return high, low


def fourier_table(count):
    modes = np.arange(count)[:, None]
    points = np.arange(count)[None, :]
    half = count // 2
    wave = np.where(modes <= half, modes, modes - half)
    angle = 2.0 * math.pi / count * (wave * points % count)
    scale = np.where((modes == 0) | (modes == half), math.sqrt(1.0 / count), math.sqrt(2.0 / count))
    return scale * np.where(modes <= half, np.cos(angle), np.sin(angle))


def radial_table(count):
    modes = np.arange(count)[:, None]
    points = np.arange(count)[None, :]
    weight = np.where(modes == 0, math.sqrt(1.0 / count), math.sqrt(2.0 / count))
    return weight * np.cos(math.pi * modes * (points + 0.5) / count)


def split(x):
    high = x.astype(jnp.bfloat16)
    low = (x - high.astype(jnp.float32)).astype(jnp.bfloat16)
    return high, low


def dot(a, b):
    return lax.dot_general(a, b, (((1,), (0,)), ((), ())), preferred_element_type=jnp.float32)


def product(a, b):
    return dot(a[0], b[0]) + (dot(a[0], b[1]) + dot(a[1], b[0]))


HALF = NX // 2


def radial_out(s_ref, a_ref, th_ref, tl_ref, out_ref):
    step = pl.program_id(0)
    table = th_ref[...], tl_ref[...]
    rows = out_ref.reshape(NR * 8, 128)

    def synthesize(ref):
        for i in range(0, 8, 2):
            pair = jnp.concatenate([ref[i, 0], ref[i + 1, 0]], axis=1)
            result = product(table, split(pair))
            rows[pl.ds(i, NR, stride=8), :] = result[:, :128]
            rows[pl.ds(i + 1, NR, stride=8), :] = result[:, 128:]

    pl.when(step < 2)(lambda: synthesize(s_ref))
    pl.when(step >= 2)(lambda: synthesize(a_ref))


def radial_back(in_ref, th_ref, tl_ref, out_ref):
    table = th_ref[...], tl_ref[...]
    rows = in_ref.reshape(NR * 8, 128)
    for i in range(0, 8, 2):
        pair = jnp.concatenate(
            [rows[pl.ds(i, NR, stride=8), :], rows[pl.ds(i + 1, NR, stride=8), :]], axis=1
        )
        result = product(table, split(pair))
        out_ref[i, 0] = result[:, :128]
        out_ref[i + 1, 0] = result[:, 128:]


def grid_kernel(
    in_hbm, yh_hbm, yl_hbm, eh_hbm, el_hbm, oh_hbm, ol_hbm, ph_hbm, pl_hbm, out_hbm,
    x_ref, out_ref, table_ref, high_ref, low_ref, state_ref, sems,
):
    tables = (eh_hbm, el_hbm, oh_hbm, ol_hbm, yh_hbm, yl_hbm, ph_hbm, pl_hbm)
    loads = {}
    for n, name in enumerate("eeooyypp"):
        copy = pltpu.make_async_copy(tables[n], table_ref.at[n], sems.at[n])
        loads.setdefault(name, []).append(copy)
    for field in range(2):
        for chunk in range(2):
            blocks = slice(2 * chunk, 2 * chunk + 2)
            loads[field, chunk] = [
                pltpu.make_async_copy(
                    in_hbm.at[:, blocks, field], x_ref.at[field, :, blocks],
                    sems.at[8 + 2 * field + chunk],
                )
            ]
    order = ((0, 0), "e", "o", (0, 1), "y", (1, 0), (1, 1), "p")
    for name in order:
        for copy in loads[name]:
            copy.start()

    def ready(name):
        for copy in loads[name]:
            copy.wait()

    even_table = lambda: (table_ref[0], table_ref[1])
    odd_table = lambda: (table_ref[2], table_ref[3])
    azimuth_table = lambda: (table_ref[4], table_ref[5])
    odd_back_table = lambda: (table_ref[6], table_ref[7])

    def axial_synthesis(field):
        for chunk in range(2):
            ready((field, chunk))
            parts = []
            for parity, table in enumerate((even_table, odd_table)):
                lanes = [
                    x_ref[field, :, 2 * chunk + k, parity].reshape(HALF, 128) for k in range(2)
                ]
                if field == 0 and chunk == 0:
                    ready("eo"[parity])
                parts.append(product(table(), split(jnp.concatenate(lanes, axis=1))))
            even, odd = parts
            columns = pl.ds(256 * chunk, 256)
            for k, value in enumerate((even + odd, even - odd)):
                rows = pl.ds(HALF * k, HALF)
                high_ref[rows, columns], low_ref[rows, columns] = split(value)

    def azimuth_synthesis(k):
        rows = pl.ds(HALF * k, HALF)
        return product((high_ref[rows, :], low_ref[rows, :]), azimuth_table())

    axial_synthesis(0)
    ready("y")
    for k in range(2):
        state_ref[pl.ds(HALF * k, HALF), :] = azimuth_synthesis(k)
    axial_synthesis(1)
    for k in range(2):
        rows = pl.ds(HALF * k, HALF)
        state = state_ref[rows, :]
        state_ref[rows, :] = (3.0 * state * state - 1.0) * azimuth_synthesis(k)
    first, second = pl.ds(0, HALF), pl.ds(HALF, HALF)
    stores = []
    for parity in range(2):
        for chunk in range(2):
            columns = pl.ds(256 * chunk, 256)
            upper, lower = state_ref[first, columns], state_ref[second, columns]
            if parity == 0:
                value = product(azimuth_table(), split(upper + lower))
            else:
                if chunk == 0:
                    ready("p")
                value = product(odd_back_table(), split(upper - lower))
            high_ref[first, columns], low_ref[first, columns] = split(value)
        result = product((high_ref[first, :], low_ref[first, :]), even_table())
        for k in range(4):
            out_ref[:, k, parity] = result[:, 128 * k : 128 * (k + 1)].reshape(64, 8, 128)
        copy = pltpu.make_async_copy(
            out_ref.at[:, :, parity], out_hbm.at[:, :, parity], sems.at[12 + parity]
        )
        copy.start()
        stores.append(copy)
    for copy in stores:
        copy.wait()


PARAMS = pltpu.CompilerParams(vmem_limit_bytes=56 * 2**20)


def run_radial_out(phase_field, section_cotangent):
    ch, cl = halves(np.ascontiguousarray(radial_table(NR).T))
    table = pl.BlockSpec((NR, NR), lambda g: (0, 0))
    return pl.pallas_call(
        radial_out,
        grid=(4,),
        in_specs=[
            pl.BlockSpec((8, 1, NR, 128), lambda g: (0, jnp.minimum(g, 1), 0, 0)),
            pl.BlockSpec((8, 1, NR, 128), lambda g: (0, jnp.maximum(g - 2, 0), 0, 0)),
            table,
            table,
        ],
        out_specs=pl.BlockSpec((NR, 8, 128), lambda g: (0, g, 0)),
        out_shape=jax.ShapeDtypeStruct((NR, 32, 128), jnp.float32),
        compiler_params=PARAMS,
        name="radial_out",
    )(phase_field.reshape(8, 2, NR, 128), section_cotangent.reshape(8, 2, NR, 128), ch, cl)


def run_grid(taken):
    axial = fourier_table(NX)
    y = halves(fourier_table(NY))
    e = halves(np.ascontiguousarray(axial[0::2, :HALF].T))
    o = halves(np.ascontiguousarray(axial[1::2, :HALF].T))
    p = halves(np.ascontiguousarray(axial[1::2, :HALF]) * math.sqrt(2.0))
    anywhere = pl.BlockSpec(memory_space=pl.ANY)
    return pl.pallas_call(
        grid_kernel,
        in_specs=[anywhere] * 9,
        out_specs=anywhere,
        out_shape=jax.ShapeDtypeStruct((64, 4, 2, 8, 128), jnp.float32),
        scratch_shapes=[
            pltpu.VMEM((2, 64, 4, 2, 8, 128), jnp.float32),
            pltpu.VMEM((64, 4, 2, 8, 128), jnp.float32),
            pltpu.VMEM((8, HALF, HALF), jnp.bfloat16),
            pltpu.VMEM((NX, NY), jnp.bfloat16),
            pltpu.VMEM((NX, NY), jnp.bfloat16),
            pltpu.VMEM((NX, NY), jnp.float32),
            pltpu.SemaphoreType.DMA((14,)),
        ],
        compiler_params=PARAMS,
        name="grid",
    )(taken.reshape(64, 4, 2, 2, 8, 128), *y, *e, *o, *p)


def run_radial_back(back):
    ch, cl = halves(radial_table(NR))
    table = pl.BlockSpec((NR, NR), lambda g: (0, 0))
    return pl.pallas_call(
        radial_back,
        grid=(2,),
        in_specs=[pl.BlockSpec((NR, 8, 128), lambda g: (0, g, 0)), table, table],
        out_specs=pl.BlockSpec((8, 1, NR, 128), lambda g: (0, g, 0, 0)),
        out_shape=jax.ShapeDtypeStruct((8, 2, NR, 128), jnp.float32),
        compiler_params=PARAMS,
        name="radial_back",
    )(back, ch, cl).reshape(16, NR, 128)


def exchange(x):
    return lax.all_to_all(x, BOTH, split_axis=0, concat_axis=0, tiled=True)


def per_device(phase_field, section_cotangent):
    taken = exchange(run_radial_out(phase_field, section_cotangent))
    back = exchange(run_grid(taken).reshape(NR, 16, 128))
    return run_radial_back(back)


def solution(mesh):
    spec = P("ax", None, "az")
    return jax.shard_map(
        per_device, mesh=mesh, in_specs=(spec, spec), out_specs=spec, check_vma=False
    )
```

time: 207 us -> 202 us (0.976)
  Pallas kernels: 29.5 us -> 24.5 us
    pallas_call x3, Pallas kernels: 29.5 us -> 24.5 us  [the longest x1 14.6 us: run_grid(): pl.pallas_call(grid_kernel, in_specs=[anywhere] * 9, out_specs=anywhere,...]
where the time goes in v3:
time: 202 us
  blocking collectives  177 us (88%)
  Pallas kernels  24.5 us (12%)
    all_to_all x2, blocking collectives, exchange(): return lax.all_to_all(x, BOTH, split_axis=0, concat_axis=0, tiled=True)  177 us
    pallas_call x1, Pallas kernels, run_grid(): pl.pallas_call(grid_kernel, in_specs=[anywhere] * 9, out_specs=anywhere,...  14.6 us
    pallas_call x1, Pallas kernels, run_radial_out(): pl.pallas_call(radial_out, grid=(4,), in_specs=[pl.BlockSpec((8, 1, NR, 1...  6.23 us

profile of v3, /device:TPU:1, one launch (start us, length us, event | category | flops | bytes accessed | tf_op | source)
XLA Modules:
  0.0 201.9 jit_solution(13111279324365723110)
XLA Ops:
  0.0 6.2 %radial_out.1 = f32[256,32,128]{2,1,0:T(8,128)} custom-call(f32[8,2,256,128]{3,2,1,0:T(8,128)} %bitcast.7, f32[8,2,256,128]{3,2,1,0:T(8,128)} %bitcast.8, bf16[256,256]{1,0:T(8,128)(2,1)} %constant.24.clone.th_ref, bf16[256,256]{1,0:T(8,128)(2,1)} %constant.25.clone.tl_ref), custom_call_target="tpu_custom_call" | custom-call | tf_op jit(solution)/shard_map/radial_out/pallas_call | solution.py:180
  6.2 115.8 %all_to_all.10 = f32[256,32,128]{2,1,0:T(8,128)} all-to-all(f32[256,32,128]{2,1,0:T(8,128)} %radial_out.1), channel_id=1, replica_groups=mesh['ax'=64,'az'=4] {'ax','az'}, dimensions={0} | all-to-all | bytes 8388608 | tf_op jit(solution)/shard_map/all_to_all | solution.py:237
  122.1 14.6 %grid.1 = f32[64,4,2,8,128]{4,3,2,1,0:T(8,128)} custom-call(f32[64,4,2,2,8,128]{5,4,3,2,1,0:T(8,128)} %bitcast.5, bf16[512,512]{1,0:T(8,128)(2,1)} %constant.26.clone.yh_hbm, bf16[512,512]{1,0:T(8,128)(2,1)} %constant.27.clone.yl_hbm, bf16[512,512]{1,0:T(8,128)(2,1)} %constant.28.clone.eh_hbm, bf16[512,512]{1,0:T(8,128)(2,1)} %constant.29.clone.el_hbm, ...), custom_call_target="tpu_custom_call" | custom-call | tf_op jit(solution)/shard_map/grid/pallas_call | solution.py:203
  136.7 61.6 %all_to_all.11.in_ref = f32[256,16,128]{2,1,0:T(8,128)} all-to-all(f32[256,16,128]{2,1,0:T(8,128)} %bitcast.6), channel_id=1, replica_groups=mesh['ax'=64,'az'=4] {'ax','az'}, dimensions={0} | all-to-all | bytes 4194304 | tf_op jit(solution)/shard_map/all_to_all | solution.py:237
  198.3 3.6 %radial_back.1 = f32[8,2,256,128]{3,2,1,0:T(8,128)} custom-call(f32[256,16,128]{2,1,0:T(8,128)} %all_to_all.11.in_ref, bf16[256,256]{1,0:T(8,128)(2,1)} %constant.34.clone.th_ref, bf16[256,256]{1,0:T(8,128)(2,1)} %constant.35.clone.tl_ref), custom_call_target="tpu_custom_call" | custom-call | tf_op jit(solution)/shard_map/radial_back/pallas_call | solution.py:225

commit v4 on v3

v4 whole, which is shorter than its diff:
```python
import functools
import math

import jax
import jax.numpy as jnp
import ml_dtypes
import numpy as np
from jax import lax
from jax.experimental import pallas as pl
from jax.experimental.pallas import tpu as pltpu
from jax.sharding import PartitionSpec as P

NX = 1024
NY = 512
NR = 256
BOTH = ("ax", "az")


def halves(table):
    high = table.astype(ml_dtypes.bfloat16)
    low = (table - high.astype(np.float64)).astype(ml_dtypes.bfloat16)
    return high, low


def fourier_table(count):
    modes = np.arange(count)[:, None]
    points = np.arange(count)[None, :]
    half = count // 2
    wave = np.where(modes <= half, modes, modes - half)
    angle = 2.0 * math.pi / count * (wave * points % count)
    scale = np.where((modes == 0) | (modes == half), math.sqrt(1.0 / count), math.sqrt(2.0 / count))
    return scale * np.where(modes <= half, np.cos(angle), np.sin(angle))


def radial_table(count):
    modes = np.arange(count)[:, None]
    points = np.arange(count)[None, :]
    weight = np.where(modes == 0, math.sqrt(1.0 / count), math.sqrt(2.0 / count))
    return weight * np.cos(math.pi * modes * (points + 0.5) / count)


def split(x):
    high = x.astype(jnp.bfloat16)
    low = (x - high.astype(jnp.float32)).astype(jnp.bfloat16)
    return high, low


def dot(a, b):
    return lax.dot_general(a, b, (((1,), (0,)), ((), ())), preferred_element_type=jnp.float32)


def product(a, b):
    return dot(a[0], b[0]) + (dot(a[0], b[1]) + dot(a[1], b[0]))


HALF = NX // 2


def radial_out(s_hbm, a_hbm, th_hbm, tl_hbm, out_ref, x_ref, turn_ref, table_ref, sems):
    tables = [
        pltpu.make_async_copy(th_hbm, table_ref.at[0], sems.at[4]),
        pltpu.make_async_copy(tl_hbm, table_ref.at[1], sems.at[5]),
    ]
    loads = [
        pltpu.make_async_copy((s_hbm, a_hbm)[g // 2].at[:, g % 2], x_ref.at[g], sems.at[g])
        for g in range(4)
    ]
    for copy in (*tables, *loads):
        copy.start()
    for copy in tables:
        copy.wait()
    table = table_ref[0], table_ref[1]
    for g in range(4):
        rows = turn_ref.at[g].reshape(NR * 8, 128)
        loads[g].wait()
        for i in range(0, 8, 2):
            pair = jnp.concatenate([x_ref[g, i], x_ref[g, i + 1]], axis=1)
            result = product(table, split(pair))
            for k in range(2):
                columns = slice(128 * k, 128 * (k + 1))
                rows[pl.ds(i + k, NR, stride=8), :] = result[:, columns]
        out_ref[:, 8 * g : 8 * (g + 1), :] = turn_ref[g]


def radial_back(in_ref, th_ref, tl_ref, out_hbm, out_ref, sems):
    table = th_ref[...], tl_ref[...]
    rows = in_ref.reshape(NR * 16, 128)
    stores = []
    for parity in range(2):
        for i in range(0, 8, 2):
            lanes = [rows[pl.ds(8 * parity + i + k, NR, stride=16), :] for k in range(2)]
            result = product(table, split(jnp.concatenate(lanes, axis=1)))
            for k in range(2):
                out_ref[parity, i + k] = result[:, 128 * k : 128 * (k + 1)]
            stores.append(
                pltpu.make_async_copy(
                    out_ref.at[parity, i : i + 2], out_hbm.at[i : i + 2, parity],
                    sems.at[4 * parity + i // 2],
                )
            )
            stores[-1].start()
    for store in stores:
        store.wait()


def grid_kernel(
    in_ref, yh_ref, yl_ref, eh_ref, el_ref, oh_ref, ol_ref, ph_ref, pl_ref, out_ref,
    high_ref, low_ref, state_ref,
):
    even_table = lambda: (eh_ref[...], el_ref[...])
    odd_table = lambda: (oh_ref[...], ol_ref[...])
    azimuth_table = lambda: (yh_ref[...], yl_ref[...])
    odd_back_table = lambda: (ph_ref[...], pl_ref[...])

    def axial_synthesis(field):
        for chunk in range(2):
            parts = []
            for parity, table in enumerate((even_table, odd_table)):
                lanes = [
                    in_ref[:, 2 * chunk + k, field, parity].reshape(HALF, 128) for k in range(2)
                ]
                parts.append(product(table(), split(jnp.concatenate(lanes, axis=1))))
            even, odd = parts
            columns = pl.ds(256 * chunk, 256)
            for k, value in enumerate((even + odd, even - odd)):
                rows = pl.ds(HALF * k, HALF)
                high_ref[rows, columns], low_ref[rows, columns] = split(value)

    def azimuth_synthesis(k):
        rows = pl.ds(HALF * k, HALF)
        return product((high_ref[rows, :], low_ref[rows, :]), azimuth_table())

    axial_synthesis(0)
    for k in range(2):
        state_ref[pl.ds(HALF * k, HALF), :] = azimuth_synthesis(k)
    axial_synthesis(1)
    for k in range(2):
        rows = pl.ds(HALF * k, HALF)
        state = state_ref[rows, :]
        state_ref[rows, :] = (3.0 * state * state - 1.0) * azimuth_synthesis(k)
    first, second = pl.ds(0, HALF), pl.ds(HALF, HALF)
    for parity in range(2):
        for chunk in range(2):
            columns = pl.ds(256 * chunk, 256)
            upper, lower = state_ref[first, columns], state_ref[second, columns]
            if parity == 0:
                value = product(azimuth_table(), split(upper + lower))
            else:
                value = product(odd_back_table(), split(upper - lower))
            high_ref[first, columns], low_ref[first, columns] = split(value)
        result = product((high_ref[first, :], low_ref[first, :]), even_table())
        for k in range(4):
            out_ref[:, k, parity] = result[:, 128 * k : 128 * (k + 1)].reshape(64, 8, 128)


def params(mebibytes):
    return pltpu.CompilerParams(vmem_limit_bytes=mebibytes * 2**20)


NEAR = pl.BlockSpec(memory_space=pltpu.VMEM)


FAR = pl.BlockSpec(memory_space=pl.ANY)


def far(x):
    return pltpu.with_memory_space_constraint(x, pltpu.HBM)


def near_shape(*dims):
    return pltpu.VMEM(dims, jnp.float32)


def run_radial_out(phase_field, section_cotangent):
    c = halves(np.ascontiguousarray(radial_table(NR).T))
    return pl.pallas_call(
        radial_out,
        in_specs=[FAR] * 4,
        out_specs=NEAR,
        out_shape=near_shape(NR, 32, 128),
        scratch_shapes=[
            pltpu.VMEM((4, 8, NR, 128), jnp.float32),
            pltpu.VMEM((4, NR, 8, 128), jnp.float32),
            pltpu.VMEM((2, NR, NR), jnp.bfloat16),
            pltpu.SemaphoreType.DMA((6,)),
        ],
        compiler_params=params(20),
        name="radial_out",
    )(*(far(x) for x in (phase_field.reshape(8, 2, NR, 128), section_cotangent.reshape(8, 2, NR, 128), *c)))


def run_grid(taken):
    axial = fourier_table(NX)
    y = halves(fourier_table(NY))
    e = halves(np.ascontiguousarray(axial[0::2, :HALF].T))
    o = halves(np.ascontiguousarray(axial[1::2, :HALF].T))
    p = halves(np.ascontiguousarray(axial[1::2, :HALF]) * math.sqrt(2.0))
    return pl.pallas_call(
        grid_kernel,
        in_specs=[NEAR] * 9,
        out_specs=NEAR,
        out_shape=near_shape(64, 4, 2, 8, 128),
        scratch_shapes=[
            pltpu.VMEM((NX, NY), jnp.bfloat16),
            pltpu.VMEM((NX, NY), jnp.bfloat16),
            pltpu.VMEM((NX, NY), jnp.float32),
        ],
        compiler_params=params(30),
        name="grid",
    )(taken.reshape(64, 4, 2, 2, 8, 128), *y, *e, *o, *p)


def run_radial_back(back):
    c = halves(radial_table(NR))
    return pl.pallas_call(
        radial_back,
        in_specs=[NEAR] * 3,
        out_specs=FAR,
        out_shape=jax.ShapeDtypeStruct((8, 2, NR, 128), jnp.float32),
        scratch_shapes=[pltpu.VMEM((2, 8, NR, 128), jnp.float32), pltpu.SemaphoreType.DMA((8,))],
        compiler_params=params(14),
        name="radial_back",
    )(back, *c).reshape(16, NR, 128)


def exchange(x):
    return lax.all_to_all(x, BOTH, split_axis=0, concat_axis=0, tiled=True)


def per_device(phase_field, section_cotangent):
    taken = exchange(run_radial_out(phase_field, section_cotangent))
    back = exchange(run_grid(taken).reshape(NR, 16, 128))
    return run_radial_back(back)


def solution(mesh):
    spec = P("ax", None, "az")
    return jax.shard_map(
        per_device, mesh=mesh, in_specs=(spec, spec), out_specs=spec, check_vma=False
    )
```

time: 202 us -> 193 us (0.955)
  Pallas kernels: 24.5 us -> 16.9 us
    pallas_call x3, Pallas kernels: 24.5 us -> 16.9 us  [the longest x1 10.2 us: run_grid(): pl.pallas_call(grid_kernel, in_specs=[NEAR] * 9, out_specs=NEAR, out_shap...]
where the time goes in v4:
time: 193 us
  blocking collectives  176 us (91%)
  Pallas kernels  16.9 us (9%)
    all_to_all x2, blocking collectives, exchange(): return lax.all_to_all(x, BOTH, split_axis=0, concat_axis=0, tiled=True)  176 us
    pallas_call x1, Pallas kernels, run_grid(): pl.pallas_call(grid_kernel, in_specs=[NEAR] * 9, out_specs=NEAR, out_shap...  10.2 us
    pallas_call x1, Pallas kernels, run_radial_out(): pl.pallas_call(radial_out, in_specs=[FAR] * 4, out_specs=NEAR, out_shape=...  4.42 us

profile of v4, /device:TPU:1, one launch (start us, length us, event | category | flops | bytes accessed | tf_op | source)
XLA Modules:
  0.0 192.8 jit_solution(8017501258432946967)
XLA Ops:
  0.0 4.4 %radial_out.1 = f32[256,32,128]{2,1,0:T(8,128)S(1)} custom-call(f32[8,2,256,128]{3,2,1,0:T(8,128)} %bitcast.7, f32[8,2,256,128]{3,2,1,0:T(8,128)} %bitcast.8, bf16[256,256]{1,0:T(8,128)(2,1)} %constant.24.clone.th_hbm, bf16[256,256]{1,0:T(8,128)(2,1)} %constant.25.clone.tl_hbm), custom_call_target="tpu_custom_call" | custom-call | tf_op jit(solution)/shard_map/radial_out/pallas_call | solution.py:176
  4.4 0.0 copy-start
  4.4 0.0 copy-start.1
  4.5 0.0 copy-start.2
  4.5 0.0 copy-start.3
  4.5 0.0 copy-start.4
  4.5 0.0 copy-start.5
  4.5 0.0 copy-start.6
  4.5 0.0 copy-start.7
  4.5 115.5 %all_to_all.10 = f32[256,32,128]{2,1,0:T(8,128)S(1)} all-to-all(f32[256,32,128]{2,1,0:T(8,128)S(1)} %radial_out.1), channel_id=1, replica_groups=mesh['ax'=64,'az'=4] {'ax','az'}, dimensions={0} | all-to-all | bytes 8388608 | tf_op jit(solution)/shard_map/all_to_all | solution.py:227
  120.1 0.0 copy-done
  120.1 0.0 copy-done.1
  120.1 0.0 copy-done.2
  120.1 0.0 copy-done.3
  120.1 0.0 copy-done.4
  120.1 0.0 copy-done.5
  120.1 0.0 copy-done.6
  120.1 0.0 copy-done.7
  120.1 10.2 %grid.1 = f32[64,4,2,8,128]{4,3,2,1,0:T(8,128)S(1)} custom-call(f32[64,4,2,2,8,128]{5,4,3,2,1,0:T(8,128)S(1)} %bitcast.5, bf16[512,512]{1,0:T(8,128)(2,1)S(1)} %copy-done.7, bf16[512,512]{1,0:T(8,128)(2,1)S(1)} %copy-done.6, bf16[512,512]{1,0:T(8,128)(2,1)S(1)} %copy-done.5, bf16[512,512]{1,0:T(8,128)(2,1)S(1)} %copy-done.4, bf16[512,512]{1,0:T(8,128)(2,1)S(1)} %copy-done.3, ...), custom_call_target="tpu_custom_call" | custom-call | tf_op jit(solution)/shard_map/grid/pallas_call | solution.py:198
  130.3 0.0 copy-start.8
  130.3 0.0 copy-start.9
  130.3 60.2 %all_to_all.11.in_ref = f32[256,16,128]{2,1,0:T(8,128)S(1)} all-to-all(f32[256,16,128]{2,1,0:T(8,128)S(1)} %bitcast.6), channel_id=1, replica_groups=mesh['ax'=64,'az'=4] {'ax','az'}, dimensions={0} | all-to-all | bytes 4194304 | tf_op jit(solution)/shard_map/all_to_all | solution.py:227
  190.5 0.0 copy-done.8
  190.5 0.0 copy-done.9
  190.5 2.3 %radial_back.1 = f32[8,2,256,128]{3,2,1,0:T(8,128)} custom-call(f32[256,16,128]{2,1,0:T(8,128)S(1)} %all_to_all.11.in_ref, bf16[256,256]{1,0:T(8,128)(2,1)S(1)} %copy-done.9, bf16[256,256]{1,0:T(8,128)(2,1)S(1)} %copy-done.8), custom_call_target="tpu_custom_call" | custom-call | tf_op jit(solution)/shard_map/radial_back/pallas_call | solution.py:215
Async XLA Ops:
  4.4 115.6 %copy-start = (bf16[512,512]{1,0:T(8,128)(2,1)S(1)}, bf16[512,512]{1,0:T(8,128)(2,1)}, u32[]{:S(2)}) copy-start(bf16[512,512]{1,0:T(8,128)(2,1)} %constant.33.clone.pl_ref) | copy-start | bytes 1572868
  4.4 115.6 %copy-start.1 = (bf16[512,512]{1,0:T(8,128)(2,1)S(1)}, bf16[512,512]{1,0:T(8,128)(2,1)}, u32[]{:S(2)}) copy-start(bf16[512,512]{1,0:T(8,128)(2,1)} %constant.32.clone.ph_ref) | copy-start | bytes 1572868
  4.5 115.6 %copy-start.2 = (bf16[512,512]{1,0:T(8,128)(2,1)S(1)}, bf16[512,512]{1,0:T(8,128)(2,1)}, u32[]{:S(2)}) copy-start(bf16[512,512]{1,0:T(8,128)(2,1)} %constant.31.clone.ol_ref) | copy-start | bytes 1572868
  4.5 115.6 %copy-start.3 = (bf16[512,512]{1,0:T(8,128)(2,1)S(1)}, bf16[512,512]{1,0:T(8,128)(2,1)}, u32[]{:S(2)}) copy-start(bf16[512,512]{1,0:T(8,128)(2,1)} %constant.30.clone.oh_ref) | copy-start | bytes 1572868
  4.5 115.6 %copy-start.4 = (bf16[512,512]{1,0:T(8,128)(2,1)S(1)}, bf16[512,512]{1,0:T(8,128)(2,1)}, u32[]{:S(2)}) copy-start(bf16[512,512]{1,0:T(8,128)(2,1)} %constant.29.clone.el_ref) | copy-start | bytes 1572868
  4.5 115.6 %copy-start.5 = (bf16[512,512]{1,0:T(8,128)(2,1)S(1)}, bf16[512,512]{1,0:T(8,128)(2,1)}, u32[]{:S(2)}) copy-start(bf16[512,512]{1,0:T(8,128)(2,1)} %constant.28.clone.eh_ref) | copy-start | bytes 1572868
  4.5 115.6 %copy-start.6 = (bf16[512,512]{1,0:T(8,128)(2,1)S(1)}, bf16[512,512]{1,0:T(8,128)(2,1)}, u32[]{:S(2)}) copy-start(bf16[512,512]{1,0:T(8,128)(2,1)} %constant.27.clone.yl_ref) | copy-start | bytes 1572868
  4.5 115.6 %copy-start.7 = (bf16[512,512]{1,0:T(8,128)(2,1)S(1)}, bf16[512,512]{1,0:T(8,128)(2,1)}, u32[]{:S(2)}) copy-start(bf16[512,512]{1,0:T(8,128)(2,1)} %constant.26.clone.yh_ref) | copy-start | bytes 1572868
  130.3 60.2 %copy-start.8 = (bf16[256,256]{1,0:T(8,128)(2,1)S(1)}, bf16[256,256]{1,0:T(8,128)(2,1)}, u32[]{:S(2)}) copy-start(bf16[256,256]{1,0:T(8,128)(2,1)} %constant.35.clone.tl_ref) | copy-start | bytes 393220
  130.3 60.2 %copy-start.9 = (bf16[256,256]{1,0:T(8,128)(2,1)S(1)}, bf16[256,256]{1,0:T(8,128)(2,1)}, u32[]{:S(2)}) copy-start(bf16[256,256]{1,0:T(8,128)(2,1)} %constant.34.clone.th_ref) | copy-start | bytes 393220

commit v5 on v4

--- a/solution.py
+++ b/solution.py
@@ -54,6 +54,7 @@
 
 
 HALF = NX // 2
+QUARTER = NX // 4
 
 
 def radial_out(s_hbm, a_hbm, th_hbm, tl_hbm, out_ref, x_ref, turn_ref, table_ref, sems):
@@ -103,32 +104,58 @@
         store.wait()
 
 
+def axial_tables():
+    axial = fourier_table(NX)
+    r = np.arange(QUARTER)
+    turned = np.where(r == 0, QUARTER, r)
+    even, odd = axial[0::2], axial[1::2]
+    even_sines = even[QUARTER:, :QUARTER].T.copy()
+    even_sines[:, 0] = 0.0
+    return even[:QUARTER, :QUARTER].T, even_sines, odd[:QUARTER, :QUARTER].T, odd[QUARTER:][:, turned].T
+
+
 def grid_kernel(
-    in_ref, yh_ref, yl_ref, eh_ref, el_ref, oh_ref, ol_ref, ph_ref, pl_ref, out_ref,
+    in_ref, yh_ref, yl_ref, eh_ref, el_ref, out_table_ref, back_table_ref, out_ref,
     high_ref, low_ref, state_ref,
 ):
-    even_table = lambda: (eh_ref[...], el_ref[...])
-    odd_table = lambda: (oh_ref[...], ol_ref[...])
-    azimuth_table = lambda: (yh_ref[...], yl_ref[...])
-    odd_back_table = lambda: (ph_ref[...], pl_ref[...])
+    index = lax.broadcasted_iota(jnp.int32, (QUARTER, 256), 0)
+    zero = index == 0
+    sign = jnp.where(index % 2 == 0, 1.0, -1.0)
+    unit = math.sqrt(1.0 / NX)
+    scale = sign * jnp.where(zero, unit, math.sqrt(2.0) * unit)
+
+    def total(x):
+        return jnp.sum(x, axis=0, keepdims=True)
 
     def axial_synthesis(field):
         for chunk in range(2):
-            parts = []
-            for parity, table in enumerate((even_table, odd_table)):
-                lanes = [
-                    in_ref[:, 2 * chunk + k, field, parity].reshape(HALF, 128) for k in range(2)
-                ]
-                parts.append(product(table(), split(jnp.concatenate(lanes, axis=1))))
-            even, odd = parts
+            modes = []
+            for parity in range(2):
+                for part in range(2):
+                    axes = slice(32 * part, 32 * (part + 1))
+                    lanes = [
+                        in_ref[axes, 2 * chunk + k, field, parity].reshape(QUARTER, 128)
+                        for k in range(2)
+                    ]
+                    modes.append(jnp.concatenate(lanes, axis=1))
+            ec, es, oc, os = (
+                product((out_table_ref[t, 0], out_table_ref[t, 1]), split(modes[t]))
+                for t in range(4)
+            )
+            nyquist = modes[1][0:1] * unit
+            middle = total(modes[0] * scale) + nyquist
+            ec = ec + sign * nyquist
+            even = ec + es, jnp.where(zero, middle, ec - es)
+            odd = jnp.where(zero, oc, os + oc), jnp.where(zero, os, os - oc)
             columns = pl.ds(256 * chunk, 256)
-            for k, value in enumerate((even + odd, even - odd)):
-                rows = pl.ds(HALF * k, HALF)
+            blocks = even[0] + odd[0], even[1] + odd[1], even[0] - odd[0], even[1] - odd[1]
+            for k, value in enumerate(blocks):
+                rows = pl.ds(QUARTER * k, QUARTER)
                 high_ref[rows, columns], low_ref[rows, columns] = split(value)
 
     def azimuth_synthesis(k):
         rows = pl.ds(HALF * k, HALF)
-        return product((high_ref[rows, :], low_ref[rows, :]), azimuth_table())
+        return product((high_ref[rows, :], low_ref[rows, :]), (yh_ref[...], yl_ref[...]))
 
     axial_synthesis(0)
     for k in range(2):
@@ -138,17 +165,32 @@
         rows = pl.ds(HALF * k, HALF)
         state = state_ref[rows, :]
         state_ref[rows, :] = (3.0 * state * state - 1.0) * azimuth_synthesis(k)
-    first, second = pl.ds(0, HALF), pl.ds(HALF, HALF)
+
+    root = math.sqrt(2.0)
+
+    def back(t, x):
+        return product((back_table_ref[t, 0], back_table_ref[t, 1]), split(x))
+
     for parity in range(2):
         for chunk in range(2):
             columns = pl.ds(256 * chunk, 256)
-            upper, lower = state_ref[first, columns], state_ref[second, columns]
+            w = [state_ref[pl.ds(QUARTER * k, QUARTER), columns] for k in range(4)]
             if parity == 0:
-                value = product(azimuth_table(), split(upper + lower))
+                upper, lower = w[0] + w[2], w[1] + w[3]
+                middle = lower[0:1]
+                folded = jnp.where(zero, upper, upper + lower)
+                cosines = back(0, folded) + (root * scale) * middle
+                nyquist = (root * unit) * (total(sign * folded) + middle)
+                sines = jnp.where(zero, nyquist, back(1, upper - lower))
             else:
-                value = product(odd_back_table(), split(upper - lower))
-            high_ref[first, columns], low_ref[first, columns] = split(value)
-        result = product((high_ref[first, :], low_ref[first, :]), even_table())
+                upper, lower = w[0] - w[2], w[1] - w[3]
+                cosines = back(2, jnp.where(zero, upper, upper - lower))
+                sines = back(3, jnp.where(zero, lower, upper + lower))
+            for k, value in enumerate((cosines, sines)):
+                rows = pl.ds(QUARTER * k, QUARTER)
+                high_ref[rows, columns], low_ref[rows, columns] = split(value)
+        first = pl.ds(0, HALF)
+        result = product((high_ref[first, :], low_ref[first, :]), (eh_ref[...], el_ref[...]))
         for k in range(4):
             out_ref[:, k, parity] = result[:, 128 * k : 128 * (k + 1)].reshape(64, 8, 128)
 
@@ -186,18 +228,19 @@
         ],
         compiler_params=params(20),
         name="radial_out",
-    )(*(far(x) for x in (phase_field.reshape(8, 2, NR, 128), section_cotangent.reshape(8, 2, NR, 128), *c)))
+    )(*(far(x.reshape(8, 2, NR, 128)) for x in (phase_field, section_cotangent)), *map(far, c))
 
 
 def run_grid(taken):
-    axial = fourier_table(NX)
-    y = halves(fourier_table(NY))
-    e = halves(np.ascontiguousarray(axial[0::2, :HALF].T))
-    o = halves(np.ascontiguousarray(axial[1::2, :HALF].T))
-    p = halves(np.ascontiguousarray(axial[1::2, :HALF]) * math.sqrt(2.0))
+    azimuth = fourier_table(NY)
+    y = halves(azimuth)
+    e = halves(np.ascontiguousarray(azimuth.T) * math.sqrt(0.5))
+    tables = axial_tables()
+    out = np.stack([np.stack(halves(t)) for t in tables])
+    back = np.stack([np.stack(halves(t.T * math.sqrt(2.0))) for t in tables])
     return pl.pallas_call(
         grid_kernel,
-        in_specs=[NEAR] * 9,
+        in_specs=[NEAR] * 7,
         out_specs=NEAR,
         out_shape=near_shape(64, 4, 2, 8, 128),
         scratch_shapes=[
@@ -207,7 +250,7 @@
         ],
         compiler_params=params(30),
         name="grid",
-    )(taken.reshape(64, 4, 2, 2, 8, 128), *y, *e, *o, *p)
+    )(taken.reshape(64, 4, 2, 2, 8, 128), *y, *e, out, back)
 
 
 def run_radial_back(back):

time: 193 us -> 191 us (0.990)
  Pallas kernels: 16.9 us -> 14.9 us
    pallas_call x1, Pallas kernels: 10.2 us -> 8.18 us  [run_grid(): pl.pallas_call(grid_kernel, in_specs=[NEAR] * 7, out_specs=NEAR, out_shap...]
where the time goes in v5:
time: 191 us
  blocking collectives  176 us (92%)
  Pallas kernels  14.9 us (8%)
    all_to_all x2, blocking collectives, exchange(): return lax.all_to_all(x, BOTH, split_axis=0, concat_axis=0, tiled=True)  176 us
    pallas_call x1, Pallas kernels, run_grid(): pl.pallas_call(grid_kernel, in_specs=[NEAR] * 7, out_specs=NEAR, out_shap...  8.18 us
    pallas_call x1, Pallas kernels, run_radial_out(): pl.pallas_call(radial_out, in_specs=[FAR] * 4, out_specs=NEAR, out_shape=...  4.42 us

profile of v5, /device:TPU:1, one launch (start us, length us, event | category | flops | bytes accessed | tf_op | source)
XLA Modules:
  0.0 190.8 jit_solution(1348013897887671787)
XLA Ops:
  0.0 4.4 %radial_out.1 = f32[256,32,128]{2,1,0:T(8,128)S(1)} custom-call(f32[8,2,256,128]{3,2,1,0:T(8,128)} %bitcast.7, f32[8,2,256,128]{3,2,1,0:T(8,128)} %bitcast.8, bf16[256,256]{1,0:T(8,128)(2,1)} %constant.20.clone.th_hbm, bf16[256,256]{1,0:T(8,128)(2,1)} %constant.21.clone.tl_hbm), custom_call_target="tpu_custom_call" | custom-call | tf_op jit(solution)/shard_map/radial_out/pallas_call | solution.py:218
  4.4 0.0 copy-start
  4.4 0.0 copy-start.1
  4.5 0.0 copy-start.2
  4.5 0.0 copy-start.3
  4.5 0.0 copy-start.4
  4.5 0.0 copy-start.5
  4.5 115.5 %all_to_all.10 = f32[256,32,128]{2,1,0:T(8,128)S(1)} all-to-all(f32[256,32,128]{2,1,0:T(8,128)S(1)} %radial_out.1), channel_id=1, replica_groups=mesh['ax'=64,'az'=4] {'ax','az'}, dimensions={0} | all-to-all | bytes 8388608 | tf_op jit(solution)/shard_map/all_to_all | solution.py:270
  120.0 0.0 copy-done
  120.0 0.0 copy-done.1
  120.0 0.0 copy-done.2
  120.0 0.0 copy-done.3
  120.1 0.0 copy-done.4
  120.1 0.0 copy-done.5
  120.1 8.2 %grid.1 = f32[64,4,2,8,128]{4,3,2,1,0:T(8,128)S(1)} custom-call(f32[64,4,2,2,8,128]{5,4,3,2,1,0:T(8,128)S(1)} %bitcast.5, bf16[512,512]{1,0:T(8,128)(2,1)S(1)} %copy-done.5, bf16[512,512]{1,0:T(8,128)(2,1)S(1)} %copy-done.4, bf16[512,512]{1,0:T(8,128)(2,1)S(1)} %copy-done.3, bf16[512,512]{1,0:T(8,128)(2,1)S(1)} %copy-done.2, ...), custom_call_target="tpu_custom_call" | custom-call | tf_op jit(solution)/shard_map/grid/pallas_call | solution.py:241
  128.3 0.0 copy-start.6
  128.3 0.0 copy-start.7
  128.3 60.2 %all_to_all.11.in_ref = f32[256,16,128]{2,1,0:T(8,128)S(1)} all-to-all(f32[256,16,128]{2,1,0:T(8,128)S(1)} %bitcast.6), channel_id=1, replica_groups=mesh['ax'=64,'az'=4] {'ax','az'}, dimensions={0} | all-to-all | bytes 4194304 | tf_op jit(solution)/shard_map/all_to_all | solution.py:270
  188.5 0.0 copy-done.6
  188.5 0.0 copy-done.7
  188.5 2.3 %radial_back.1 = f32[8,2,256,128]{3,2,1,0:T(8,128)} custom-call(f32[256,16,128]{2,1,0:T(8,128)S(1)} %all_to_all.11.in_ref, bf16[256,256]{1,0:T(8,128)(2,1)S(1)} %copy-done.7, bf16[256,256]{1,0:T(8,128)(2,1)S(1)} %copy-done.6), custom_call_target="tpu_custom_call" | custom-call | tf_op jit(solution)/shard_map/radial_back/pallas_call | solution.py:258
Async XLA Ops:
  4.4 115.6 %copy-start = (bf16[4,2,256,256]{3,2,1,0:T(8,128)(2,1)S(1)}, bf16[4,2,256,256]{3,2,1,0:T(8,128)(2,1)}, u32[]{:S(2)}) copy-start(bf16[4,2,256,256]{3,2,1,0:T(8,128)(2,1)} %constant.27.clone.back_table_ref) | copy-start | bytes 3145732
  4.4 115.6 %copy-start.1 = (bf16[4,2,256,256]{3,2,1,0:T(8,128)(2,1)S(1)}, bf16[4,2,256,256]{3,2,1,0:T(8,128)(2,1)}, u32[]{:S(2)}) copy-start(bf16[4,2,256,256]{3,2,1,0:T(8,128)(2,1)} %constant.26.clone.out_table_ref) | copy-start | bytes 3145732
  4.5 115.6 %copy-start.2 = (bf16[512,512]{1,0:T(8,128)(2,1)S(1)}, bf16[512,512]{1,0:T(8,128)(2,1)}, u32[]{:S(2)}) copy-start(bf16[512,512]{1,0:T(8,128)(2,1)} %constant.25.clone.el_ref) | copy-start | bytes 1572868
  4.5 115.6 %copy-start.3 = (bf16[512,512]{1,0:T(8,128)(2,1)S(1)}, bf16[512,512]{1,0:T(8,128)(2,1)}, u32[]{:S(2)}) copy-start(bf16[512,512]{1,0:T(8,128)(2,1)} %constant.24.clone.eh_ref) | copy-start | bytes 1572868
  4.5 115.6 %copy-start.4 = (bf16[512,512]{1,0:T(8,128)(2,1)S(1)}, bf16[512,512]{1,0:T(8,128)(2,1)}, u32[]{:S(2)}) copy-start(bf16[512,512]{1,0:T(8,128)(2,1)} %constant.23.clone.yl_ref) | copy-start | bytes 1572868
  4.5 115.6 %copy-start.5 = (bf16[512,512]{1,0:T(8,128)(2,1)S(1)}, bf16[512,512]{1,0:T(8,128)(2,1)}, u32[]{:S(2)}) copy-start(bf16[512,512]{1,0:T(8,128)(2,1)} %constant.22.clone.yh_ref) | copy-start | bytes 1572868
  128.3 60.2 %copy-start.6 = (bf16[256,256]{1,0:T(8,128)(2,1)S(1)}, bf16[256,256]{1,0:T(8,128)(2,1)}, u32[]{:S(2)}) copy-start(bf16[256,256]{1,0:T(8,128)(2,1)} %constant.29.clone.tl_ref) | copy-start | bytes 393220
  128.3 60.2 %copy-start.7 = (bf16[256,256]{1,0:T(8,128)(2,1)S(1)}, bf16[256,256]{1,0:T(8,128)(2,1)}, u32[]{:S(2)}) copy-start(bf16[256,256]{1,0:T(8,128)(2,1)} %constant.28.clone.th_ref) | copy-start | bytes 393220

commit v6 on v5

--- a/solution.py
+++ b/solution.py
@@ -114,15 +114,32 @@
     return even[:QUARTER, :QUARTER].T, even_sines, odd[:QUARTER, :QUARTER].T, odd[QUARTER:][:, turned].T
 
 
+def azimuth_tables():
+    table = fourier_table(NY)
+    half = NY // 2
+    sines = table[half:, :half].copy()
+    sines[0] = 0.0
+    return table[:half, :half], sines
+
+
 def grid_kernel(
-    in_ref, yh_ref, yl_ref, eh_ref, el_ref, out_table_ref, back_table_ref, out_ref,
-    high_ref, low_ref, state_ref,
+    in_ref, line_out_ref, line_back_ref, out_table_ref, back_table_ref, out_ref,
+    high_ref, low_ref, state_ref, middle_ref, nyquist_ref,
 ):
     index = lax.broadcasted_iota(jnp.int32, (QUARTER, 256), 0)
     zero = index == 0
     sign = jnp.where(index % 2 == 0, 1.0, -1.0)
     unit = math.sqrt(1.0 / NX)
     scale = sign * jnp.where(zero, unit, math.sqrt(2.0) * unit)
+
+    lane = lax.broadcasted_iota(jnp.int32, (1, 256), 1)
+    lane_zero = lane == 0
+    lane_sign = jnp.where(lane % 2 == 0, 1.0, -1.0)
+    lane_unit = math.sqrt(1.0 / NY)
+    lane_scale = lane_sign * jnp.where(lane_zero, lane_unit, math.sqrt(2.0) * lane_unit)
+
+    def line_total(x):
+        return jnp.sum(x, axis=1, keepdims=True)
 
     def total(x):
         return jnp.sum(x, axis=0, keepdims=True)
@@ -152,19 +169,37 @@
             for k, value in enumerate(blocks):
                 rows = pl.ds(QUARTER * k, QUARTER)
                 high_ref[rows, columns], low_ref[rows, columns] = split(value)
+                if chunk == 0:
+                    middle_ref[rows, 0:1] = line_total(value * lane_scale)
+                else:
+                    nyquist_ref[rows, 0:1] = value[:, 0:1] * lane_unit
+
+    cosine_lanes, sine_lanes = pl.ds(0, 256), pl.ds(256, 256)
 
     def azimuth_synthesis(k):
         rows = pl.ds(HALF * k, HALF)
-        return product((high_ref[rows, :], low_ref[rows, :]), (yh_ref[...], yl_ref[...]))
+        cosines, sines = (
+            product(
+                (high_ref[rows, lanes], low_ref[rows, lanes]),
+                (line_out_ref[t, 0], line_out_ref[t, 1]),
+            )
+            for t, lanes in enumerate((cosine_lanes, sine_lanes))
+        )
+        nyquist = nyquist_ref[rows, 0:1]
+        cosines = cosines + lane_sign * nyquist
+        middle = middle_ref[rows, 0:1] + nyquist
+        return cosines + sines, jnp.where(lane_zero, middle, cosines - sines)
 
     axial_synthesis(0)
     for k in range(2):
-        state_ref[pl.ds(HALF * k, HALF), :] = azimuth_synthesis(k)
+        rows = pl.ds(HALF * k, HALF)
+        state_ref[rows, cosine_lanes], state_ref[rows, sine_lanes] = azimuth_synthesis(k)
     axial_synthesis(1)
     for k in range(2):
         rows = pl.ds(HALF * k, HALF)
-        state = state_ref[rows, :]
-        state_ref[rows, :] = (3.0 * state * state - 1.0) * azimuth_synthesis(k)
+        for lanes, adjoint in zip((cosine_lanes, sine_lanes), azimuth_synthesis(k)):
+            state = state_ref[rows, lanes]
+            state_ref[rows, lanes] = (3.0 * state * state - 1.0) * adjoint
 
     root = math.sqrt(2.0)
 
@@ -172,6 +207,7 @@
         return product((back_table_ref[t, 0], back_table_ref[t, 1]), split(x))
 
     for parity in range(2):
+        lines = []
         for chunk in range(2):
             columns = pl.ds(256 * chunk, 256)
             w = [state_ref[pl.ds(QUARTER * k, QUARTER), columns] for k in range(4)]
@@ -186,13 +222,20 @@
                 upper, lower = w[0] - w[2], w[1] - w[3]
                 cosines = back(2, jnp.where(zero, upper, upper - lower))
                 sines = back(3, jnp.where(zero, lower, upper + lower))
-            for k, value in enumerate((cosines, sines)):
-                rows = pl.ds(QUARTER * k, QUARTER)
-                high_ref[rows, columns], low_ref[rows, columns] = split(value)
-        first = pl.ds(0, HALF)
-        result = product((high_ref[first, :], low_ref[first, :]), (eh_ref[...], el_ref[...]))
-        for k in range(4):
-            out_ref[:, k, parity] = result[:, 128 * k : 128 * (k + 1)].reshape(64, 8, 128)
+            lines.append((cosines, sines))
+        for part in range(2):
+            upper, lower = lines[0][part], lines[1][part]
+            middle = lower[:, 0:1]
+            folded = jnp.where(lane_zero, upper, upper + lower)
+            cosines = product(split(folded), (line_back_ref[0, 0], line_back_ref[0, 1]))
+            cosines = cosines + (lane_scale / root) * middle
+            nyquist = (lane_unit / root) * (line_total(lane_sign * folded) + middle)
+            sines = product(split(upper - lower), (line_back_ref[1, 0], line_back_ref[1, 1]))
+            sines = jnp.where(lane_zero, nyquist, sines)
+            for k in range(4):
+                value = (cosines, sines)[k // 2][:, 128 * (k % 2) : 128 * (k % 2 + 1)]
+                axes = slice(32 * part, 32 * (part + 1))
+                out_ref[axes, k, parity] = value.reshape(32, 8, 128)
 
 
 def params(mebibytes):
@@ -232,25 +275,25 @@
 
 
 def run_grid(taken):
-    azimuth = fourier_table(NY)
-    y = halves(azimuth)
-    e = halves(np.ascontiguousarray(azimuth.T) * math.sqrt(0.5))
-    tables = axial_tables()
-    out = np.stack([np.stack(halves(t)) for t in tables])
-    back = np.stack([np.stack(halves(t.T * math.sqrt(2.0))) for t in tables])
+    tables = []
+    for group, factor in ((azimuth_tables(), math.sqrt(0.5)), (axial_tables(), math.sqrt(2.0))):
+        tables.append(np.stack([np.stack(halves(t)) for t in group]))
+        tables.append(np.stack([np.stack(halves(t.T * factor)) for t in group]))
     return pl.pallas_call(
         grid_kernel,
-        in_specs=[NEAR] * 7,
+        in_specs=[NEAR] * 5,
         out_specs=NEAR,
         out_shape=near_shape(64, 4, 2, 8, 128),
         scratch_shapes=[
             pltpu.VMEM((NX, NY), jnp.bfloat16),
             pltpu.VMEM((NX, NY), jnp.bfloat16),
             pltpu.VMEM((NX, NY), jnp.float32),
+            pltpu.VMEM((NX, 128), jnp.float32),
+            pltpu.VMEM((NX, 128), jnp.float32),
         ],
         compiler_params=params(30),
         name="grid",
-    )(taken.reshape(64, 4, 2, 2, 8, 128), *y, *e, out, back)
+    )(taken.reshape(64, 4, 2, 2, 8, 128), *tables)
 
 
 def run_radial_back(back):

time: 191 us -> 189 us (0.990)
  no operation moved by 1% of the time
where the time goes in v6:
time: 189 us
  blocking collectives  176 us (93%)
  Pallas kernels  13.4 us (7%)
    all_to_all x2, blocking collectives, exchange(): return lax.all_to_all(x, BOTH, split_axis=0, concat_axis=0, tiled=True)  176 us
    pallas_call x1, Pallas kernels, run_grid(): pl.pallas_call(grid_kernel, in_specs=[NEAR] * 5, out_specs=NEAR, out_shap...  6.69 us
    pallas_call x1, Pallas kernels, run_radial_out(): pl.pallas_call(radial_out, in_specs=[FAR] * 4, out_specs=NEAR, out_shape=...  4.42 us

profile of v6, /device:TPU:1, one launch (start us, length us, event | category | flops | bytes accessed | tf_op | source)
XLA Modules:
  0.0 189.2 jit_solution(2401132601155840204)
XLA Ops:
  0.0 4.4 %radial_out.1 = f32[256,32,128]{2,1,0:T(8,128)S(1)} custom-call(f32[8,2,256,128]{3,2,1,0:T(8,128)} %bitcast.7, f32[8,2,256,128]{3,2,1,0:T(8,128)} %bitcast.8, bf16[256,256]{1,0:T(8,128)(2,1)} %constant.16.clone.th_hbm, bf16[256,256]{1,0:T(8,128)(2,1)} %constant.17.clone.tl_hbm), custom_call_target="tpu_custom_call" | custom-call | tf_op jit(solution)/shard_map/radial_out/pallas_call | solution.py:261
  4.4 0.0 copy-start
  4.4 0.0 copy-start.1
  4.5 0.0 copy-start.2
  4.5 0.0 copy-start.3
  4.5 115.5 %all_to_all.10 = f32[256,32,128]{2,1,0:T(8,128)S(1)} all-to-all(f32[256,32,128]{2,1,0:T(8,128)S(1)} %radial_out.1), channel_id=1, replica_groups=mesh['ax'=64,'az'=4] {'ax','az'}, dimensions={0} | all-to-all | bytes 8388608 | tf_op jit(solution)/shard_map/all_to_all | solution.py:313
  120.0 0.0 copy-done
  120.0 0.0 copy-done.1
  120.0 0.0 copy-done.2
  120.0 0.0 copy-done.3
  120.0 6.7 %grid.1 = f32[64,4,2,8,128]{4,3,2,1,0:T(8,128)S(1)} custom-call(f32[64,4,2,2,8,128]{5,4,3,2,1,0:T(8,128)S(1)} %bitcast.5, bf16[2,2,256,256]{3,2,1,0:T(8,128)(2,1)S(1)} %copy-done.3, bf16[2,2,256,256]{3,2,1,0:T(8,128)(2,1)S(1)} %copy-done.2, bf16[4,2,256,256]{3,2,1,0:T(8,128)(2,1)S(1)} %copy-done.1, bf16[4,2,256,256]{3,2,1,0:T(8,128)(2,1)S(1)} %copy-done), custom_call_target="tpu_custom_call" | custom-call | tf_op jit(solution)/shard_map/grid/pallas_call | solution.py:282
  126.7 0.0 copy-start.4
  126.7 0.0 copy-start.5
  126.8 60.2 %all_to_all.11.in_ref = f32[256,16,128]{2,1,0:T(8,128)S(1)} all-to-all(f32[256,16,128]{2,1,0:T(8,128)S(1)} %bitcast.6), channel_id=1, replica_groups=mesh['ax'=64,'az'=4] {'ax','az'}, dimensions={0} | all-to-all | bytes 4194304 | tf_op jit(solution)/shard_map/all_to_all | solution.py:313
  186.9 0.0 copy-done.4
  186.9 0.0 copy-done.5
  186.9 2.3 %radial_back.1 = f32[8,2,256,128]{3,2,1,0:T(8,128)} custom-call(f32[256,16,128]{2,1,0:T(8,128)S(1)} %all_to_all.11.in_ref, bf16[256,256]{1,0:T(8,128)(2,1)S(1)} %copy-done.5, bf16[256,256]{1,0:T(8,128)(2,1)S(1)} %copy-done.4), custom_call_target="tpu_custom_call" | custom-call | tf_op jit(solution)/shard_map/radial_back/pallas_call | solution.py:301
Async XLA Ops:
  4.4 115.6 %copy-start = (bf16[4,2,256,256]{3,2,1,0:T(8,128)(2,1)S(1)}, bf16[4,2,256,256]{3,2,1,0:T(8,128)(2,1)}, u32[]{:S(2)}) copy-start(bf16[4,2,256,256]{3,2,1,0:T(8,128)(2,1)} %constant.21.clone.back_table_ref) | copy-start | bytes 3145732
  4.4 115.6 %copy-start.1 = (bf16[4,2,256,256]{3,2,1,0:T(8,128)(2,1)S(1)}, bf16[4,2,256,256]{3,2,1,0:T(8,128)(2,1)}, u32[]{:S(2)}) copy-start(bf16[4,2,256,256]{3,2,1,0:T(8,128)(2,1)} %constant.20.clone.out_table_ref) | copy-start | bytes 3145732
  4.5 115.6 %copy-start.2 = (bf16[2,2,256,256]{3,2,1,0:T(8,128)(2,1)S(1)}, bf16[2,2,256,256]{3,2,1,0:T(8,128)(2,1)}, u32[]{:S(2)}) copy-start(bf16[2,2,256,256]{3,2,1,0:T(8,128)(2,1)} %constant.19.clone.line_back_ref) | copy-start | bytes 1572868
  4.5 115.6 %copy-start.3 = (bf16[2,2,256,256]{3,2,1,0:T(8,128)(2,1)S(1)}, bf16[2,2,256,256]{3,2,1,0:T(8,128)(2,1)}, u32[]{:S(2)}) copy-start(bf16[2,2,256,256]{3,2,1,0:T(8,128)(2,1)} %constant.18.clone.line_out_ref) | copy-start | bytes 1572868
  126.7 60.2 %copy-start.4 = (bf16[256,256]{1,0:T(8,128)(2,1)S(1)}, bf16[256,256]{1,0:T(8,128)(2,1)}, u32[]{:S(2)}) copy-start(bf16[256,256]{1,0:T(8,128)(2,1)} %constant.23.clone.tl_ref) | copy-start | bytes 393220
  126.7 60.2 %copy-start.5 = (bf16[256,256]{1,0:T(8,128)(2,1)S(1)}, bf16[256,256]{1,0:T(8,128)(2,1)}, u32[]{:S(2)}) copy-start(bf16[256,256]{1,0:T(8,128)(2,1)} %constant.22.clone.th_ref) | copy-start | bytes 393220

commit v7 on v6

--- a/solution.py
+++ b/solution.py
@@ -50,7 +50,7 @@
 
 
 def product(a, b):
-    return dot(a[0], b[0]) + (dot(a[0], b[1]) + dot(a[1], b[0]))
+    return dot(jnp.concatenate([a[0], a[0], a[1]], 1), jnp.concatenate([b[0], b[1], b[0]], 0))
 
 
 HALF = NX // 2
@@ -59,28 +59,37 @@
 
 def radial_out(s_hbm, a_hbm, th_hbm, tl_hbm, out_ref, x_ref, turn_ref, table_ref, sems):
     tables = [
-        pltpu.make_async_copy(th_hbm, table_ref.at[0], sems.at[4]),
-        pltpu.make_async_copy(tl_hbm, table_ref.at[1], sems.at[5]),
+        pltpu.make_async_copy(th_hbm, table_ref.at[0], sems.at[3]),
+        pltpu.make_async_copy(tl_hbm, table_ref.at[1], sems.at[4]),
     ]
-    loads = [
-        pltpu.make_async_copy((s_hbm, a_hbm)[g // 2].at[:, g % 2], x_ref.at[g], sems.at[g])
-        for g in range(4)
-    ]
-    for copy in (*tables, *loads):
+    loads = {
+        (0, 0): pltpu.make_async_copy(s_hbm.at[0:4], x_ref.at[0, 0:4], sems.at[0]),
+        (0, 4): pltpu.make_async_copy(s_hbm.at[4:8], x_ref.at[0, 4:8], sems.at[1]),
+        (1, 0): pltpu.make_async_copy(a_hbm, x_ref.at[1], sems.at[2]),
+    }
+    for copy in (*tables, *loads.values()):
         copy.start()
     for copy in tables:
         copy.wait()
     table = table_ref[0], table_ref[1]
-    for g in range(4):
-        rows = turn_ref.at[g].reshape(NR * 8, 128)
-        loads[g].wait()
-        for i in range(0, 8, 2):
-            pair = jnp.concatenate([x_ref[g, i], x_ref[g, i + 1]], axis=1)
+
+    def turn(field, first, last):
+        for group in (2 * field, 2 * field + 1):
+            rows = slice(8 * group, 8 * (group + 1))
+            out_ref[first:last, rows, :] = turn_ref[group, first:last]
+
+    for field in range(2):
+        for i in range(8):
+            if (field, i) in loads:
+                loads[field, i].wait()
+            pair = jnp.concatenate([x_ref[field, i, 0], x_ref[field, i, 1]], axis=1)
             result = product(table, split(pair))
-            for k in range(2):
-                columns = slice(128 * k, 128 * (k + 1))
-                rows[pl.ds(i + k, NR, stride=8), :] = result[:, columns]
-        out_ref[:, 8 * g : 8 * (g + 1), :] = turn_ref[g]
+            for parity in range(2):
+                rows = turn_ref.at[2 * field + parity].reshape(NR * 8, 128)
+                rows[pl.ds(i, NR, stride=8), :] = result[:, 128 * parity : 128 * (parity + 1)]
+            if field == 1:
+                turn(0, 32 * i, 32 * (i + 1))
+    turn(1, 0, NR)
 
 
 def radial_back(in_ref, th_ref, tl_ref, out_hbm, out_ref, sems):
@@ -264,10 +273,10 @@
         out_specs=NEAR,
         out_shape=near_shape(NR, 32, 128),
         scratch_shapes=[
-            pltpu.VMEM((4, 8, NR, 128), jnp.float32),
+            pltpu.VMEM((2, 8, 2, NR, 128), jnp.float32),
             pltpu.VMEM((4, NR, 8, 128), jnp.float32),
             pltpu.VMEM((2, NR, NR), jnp.bfloat16),
-            pltpu.SemaphoreType.DMA((6,)),
+            pltpu.SemaphoreType.DMA((5,)),
         ],
         compiler_params=params(20),
         name="radial_out",

time: 189 us -> 189 us (level)
  no operation moved by 1% of the time
where the time goes in v7:
time: 189 us
  blocking collectives  176 us (93%)
  Pallas kernels  12.9 us (7%)
    all_to_all x2, blocking collectives, exchange(): return lax.all_to_all(x, BOTH, split_axis=0, concat_axis=0, tiled=True)  176 us
    pallas_call x1, Pallas kernels, run_grid(): pl.pallas_call(grid_kernel, in_specs=[NEAR] * 5, out_specs=NEAR, out_shap...  6.43 us
    pallas_call x1, Pallas kernels, run_radial_out(): pl.pallas_call(radial_out, in_specs=[FAR] * 4, out_specs=NEAR, out_shape=...  4.14 us

profile of v7, /device:TPU:1, one launch (start us, length us, event | category | flops | bytes accessed | tf_op | source)
XLA Modules:
  0.0 188.7 jit_solution(14574181767306127649)
XLA Ops:
  0.0 4.1 %radial_out.1 = f32[256,32,128]{2,1,0:T(8,128)S(1)} custom-call(f32[8,2,256,128]{3,2,1,0:T(8,128)} %bitcast.7, f32[8,2,256,128]{3,2,1,0:T(8,128)} %bitcast.8, bf16[256,256]{1,0:T(8,128)(2,1)} %constant.16.clone.th_hbm, bf16[256,256]{1,0:T(8,128)(2,1)} %constant.17.clone.tl_hbm), custom_call_target="tpu_custom_call" | custom-call | tf_op jit(solution)/shard_map/radial_out/pallas_call | solution.py:270
  4.1 0.0 copy-start
  4.2 0.0 copy-start.1
  4.2 0.0 copy-start.2
  4.2 0.0 copy-start.3
  4.2 115.5 %all_to_all.10 = f32[256,32,128]{2,1,0:T(8,128)S(1)} all-to-all(f32[256,32,128]{2,1,0:T(8,128)S(1)} %radial_out.1), channel_id=1, replica_groups=mesh['ax'=64,'az'=4] {'ax','az'}, dimensions={0} | all-to-all | bytes 8388608 | tf_op jit(solution)/shard_map/all_to_all | solution.py:322
  119.7 0.0 copy-done
  119.7 0.0 copy-done.1
  119.7 0.0 copy-done.2
  119.7 0.0 copy-done.3
  119.7 6.4 %grid.1 = f32[64,4,2,8,128]{4,3,2,1,0:T(8,128)S(1)} custom-call(f32[64,4,2,2,8,128]{5,4,3,2,1,0:T(8,128)S(1)} %bitcast.5, bf16[2,2,256,256]{3,2,1,0:T(8,128)(2,1)S(1)} %copy-done.3, bf16[2,2,256,256]{3,2,1,0:T(8,128)(2,1)S(1)} %copy-done.2, bf16[4,2,256,256]{3,2,1,0:T(8,128)(2,1)S(1)} %copy-done.1, bf16[4,2,256,256]{3,2,1,0:T(8,128)(2,1)S(1)} %copy-done), custom_call_target="tpu_custom_call" | custom-call | tf_op jit(solution)/shard_map/grid/pallas_call | solution.py:291
  126.2 0.0 copy-start.4
  126.2 0.0 copy-start.5
  126.2 60.2 %all_to_all.11.in_ref = f32[256,16,128]{2,1,0:T(8,128)S(1)} all-to-all(f32[256,16,128]{2,1,0:T(8,128)S(1)} %bitcast.6), channel_id=1, replica_groups=mesh['ax'=64,'az'=4] {'ax','az'}, dimensions={0} | all-to-all | bytes 4194304 | tf_op jit(solution)/shard_map/all_to_all | solution.py:322
  186.4 0.0 copy-done.4
  186.4 0.0 copy-done.5
  186.4 2.3 %radial_back.1 = f32[8,2,256,128]{3,2,1,0:T(8,128)} custom-call(f32[256,16,128]{2,1,0:T(8,128)S(1)} %all_to_all.11.in_ref, bf16[256,256]{1,0:T(8,128)(2,1)S(1)} %copy-done.5, bf16[256,256]{1,0:T(8,128)(2,1)S(1)} %copy-done.4), custom_call_target="tpu_custom_call" | custom-call | tf_op jit(solution)/shard_map/radial_back/pallas_call | solution.py:310
Async XLA Ops:
  4.1 115.6 %copy-start = (bf16[4,2,256,256]{3,2,1,0:T(8,128)(2,1)S(1)}, bf16[4,2,256,256]{3,2,1,0:T(8,128)(2,1)}, u32[]{:S(2)}) copy-start(bf16[4,2,256,256]{3,2,1,0:T(8,128)(2,1)} %constant.21.clone.back_table_ref) | copy-start | bytes 3145732
  4.2 115.6 %copy-start.1 = (bf16[4,2,256,256]{3,2,1,0:T(8,128)(2,1)S(1)}, bf16[4,2,256,256]{3,2,1,0:T(8,128)(2,1)}, u32[]{:S(2)}) copy-start(bf16[4,2,256,256]{3,2,1,0:T(8,128)(2,1)} %constant.20.clone.out_table_ref) | copy-start | bytes 3145732
  4.2 115.6 %copy-start.2 = (bf16[2,2,256,256]{3,2,1,0:T(8,128)(2,1)S(1)}, bf16[2,2,256,256]{3,2,1,0:T(8,128)(2,1)}, u32[]{:S(2)}) copy-start(bf16[2,2,256,256]{3,2,1,0:T(8,128)(2,1)} %constant.19.clone.line_back_ref) | copy-start | bytes 1572868
  4.2 115.6 %copy-start.3 = (bf16[2,2,256,256]{3,2,1,0:T(8,128)(2,1)S(1)}, bf16[2,2,256,256]{3,2,1,0:T(8,128)(2,1)}, u32[]{:S(2)}) copy-start(bf16[2,2,256,256]{3,2,1,0:T(8,128)(2,1)} %constant.18.clone.line_out_ref) | copy-start | bytes 1572868
  126.2 60.2 %copy-start.4 = (bf16[256,256]{1,0:T(8,128)(2,1)S(1)}, bf16[256,256]{1,0:T(8,128)(2,1)}, u32[]{:S(2)}) copy-start(bf16[256,256]{1,0:T(8,128)(2,1)} %constant.23.clone.tl_ref) | copy-start | bytes 393220
  126.2 60.2 %copy-start.5 = (bf16[256,256]{1,0:T(8,128)(2,1)S(1)}, bf16[256,256]{1,0:T(8,128)(2,1)}, u32[]{:S(2)}) copy-start(bf16[256,256]{1,0:T(8,128)(2,1)} %constant.22.clone.th_ref) | copy-start | bytes 393220

commit v8 on v7

--- a/solution.py
+++ b/solution.py
@@ -8,12 +8,13 @@
 from jax import lax
 from jax.experimental import pallas as pl
 from jax.experimental.pallas import tpu as pltpu
-from jax.sharding import PartitionSpec as P
+from jax.sharding import Mesh, PartitionSpec as P
 
 NX = 1024
 NY = 512
 NR = 256
-BOTH = ("ax", "az")
+AXES = ("x", "y", "zl", "core", "zh")
+ORDER = ("x", "y", "zh", "zl", "core")
 
 
 def halves(table):
@@ -158,9 +159,9 @@
             modes = []
             for parity in range(2):
                 for part in range(2):
-                    axes = slice(32 * part, 32 * (part + 1))
+                    axes = slice(8 * part, 8 * (part + 1))
                     lanes = [
-                        in_ref[axes, 2 * chunk + k, field, parity].reshape(QUARTER, 128)
+                        in_ref[axes, 2 * chunk + k, :, field, parity].reshape(QUARTER, 128)
                         for k in range(2)
                     ]
                     modes.append(jnp.concatenate(lanes, axis=1))
@@ -243,8 +244,8 @@
             sines = jnp.where(lane_zero, nyquist, sines)
             for k in range(4):
                 value = (cosines, sines)[k // 2][:, 128 * (k % 2) : 128 * (k % 2 + 1)]
-                axes = slice(32 * part, 32 * (part + 1))
-                out_ref[axes, k, parity] = value.reshape(32, 8, 128)
+                axes = slice(8 * part, 8 * (part + 1))
+                out_ref[axes, k, :, parity] = value.reshape(8, 4, 8, 128)
 
 
 def params(mebibytes):
@@ -292,7 +293,7 @@
         grid_kernel,
         in_specs=[NEAR] * 5,
         out_specs=NEAR,
-        out_shape=near_shape(64, 4, 2, 8, 128),
+        out_shape=near_shape(16, 4, 4, 2, 8, 128),
         scratch_shapes=[
             pltpu.VMEM((NX, NY), jnp.bfloat16),
             pltpu.VMEM((NX, NY), jnp.bfloat16),
@@ -302,7 +303,7 @@
         ],
         compiler_params=params(30),
         name="grid",
-    )(taken.reshape(64, 4, 2, 2, 8, 128), *tables)
+    )(taken.reshape(16, 4, 4, 2, 2, 8, 128), *tables)
 
 
 def run_radial_back(back):
@@ -319,7 +320,7 @@
 
 
 def exchange(x):
-    return lax.all_to_all(x, BOTH, split_axis=0, concat_axis=0, tiled=True)
+    return lax.all_to_all(x, ORDER, split_axis=0, concat_axis=0, tiled=True)
 
 
 def per_device(phase_field, section_cotangent):
@@ -329,7 +330,8 @@
 
 
 def solution(mesh):
-    spec = P("ax", None, "az")
+    names = Mesh(mesh.devices.reshape(4, 4, 2, 2, 4), AXES)
+    spec = P(("x", "y", "zl", "core"), None, "zh")
     return jax.shard_map(
-        per_device, mesh=mesh, in_specs=(spec, spec), out_specs=spec, check_vma=False
+        per_device, mesh=names, in_specs=(spec, spec), out_specs=spec, check_vma=False
     )

time: 189 us -> 188 us (level)
  blocking collectives: 176 us -> 174 us
where the time goes in v8:
time: 188 us; the launch traced here: 187 us
  blocking collectives  174 us (93%)
  Pallas kernels  12.9 us (7%)
    all_to_all x2, blocking collectives, exchange(): return lax.all_to_all(x, ORDER, split_axis=0, concat_axis=0, tiled=True)  174 us
    pallas_call x1, Pallas kernels, run_grid(): pl.pallas_call(grid_kernel, in_specs=[NEAR] * 5, out_specs=NEAR, out_shap...  6.42 us
    pallas_call x1, Pallas kernels, run_radial_out(): pl.pallas_call(radial_out, in_specs=[FAR] * 4, out_specs=NEAR, out_shape=...  4.14 us

profile of v8, /device:TPU:1, one launch (start us, length us, event | category | flops | bytes accessed | tf_op | source)
XLA Modules:
  0.0 187.4 jit_solution(3451369405107660498)
XLA Ops:
  0.0 4.1 %radial_out.1 = f32[256,32,128]{2,1,0:T(8,128)S(1)} custom-call(f32[8,2,256,128]{3,2,1,0:T(8,128)} %bitcast.7, f32[8,2,256,128]{3,2,1,0:T(8,128)} %bitcast.8, bf16[256,256]{1,0:T(8,128)(2,1)} %constant.16.clone.th_hbm, bf16[256,256]{1,0:T(8,128)(2,1)} %constant.17.clone.tl_hbm), custom_call_target="tpu_custom_call" | custom-call | tf_op jit(solution)/shard_map/radial_out/pallas_call | solution.py:271
  4.1 0.0 copy-start
  4.2 0.0 copy-start.1
  4.2 0.0 copy-start.2
  4.2 0.0 copy-start.3
  4.2 115.2 %all_to_all.10 = f32[256,32,128]{2,1,0:T(8,128)S(1)} all-to-all(f32[256,32,128]{2,1,0:T(8,128)S(1)} %radial_out.1), channel_id=1, replica_groups=mesh['x'=4,'y'=4,'zl'=2,'core'=2,'zh'=4] {'x','y','zh','zl','core'}, dimensions={0} | all-to-all | bytes 8388608 | tf_op jit(solution)/shard_map/all_to_all | solution.py:323
  119.4 0.0 copy-done
  119.4 0.0 copy-done.1
  119.4 0.0 copy-done.2
  119.4 0.0 copy-done.3
  119.4 6.4 %grid.1 = f32[16,4,4,2,8,128]{5,4,3,2,1,0:T(8,128)S(1)} custom-call(f32[16,4,4,2,2,8,128]{6,5,4,3,2,1,0:T(8,128)S(1)} %bitcast.5, bf16[2,2,256,256]{3,2,1,0:T(8,128)(2,1)S(1)} %copy-done.3, bf16[2,2,256,256]{3,2,1,0:T(8,128)(2,1)S(1)} %copy-done.2, bf16[4,2,256,256]{3,2,1,0:T(8,128)(2,1)S(1)} %copy-done.1, bf16[4,2,256,256]{3,2,1,0:T(8,128)(2,1)S(1)} %copy-done), custom_call_target="tpu_custom_call" | custom-call | tf_op jit(solution)/shard_map/grid/pallas_call | solution.py:292
  125.8 0.0 copy-start.4
  125.8 0.0 copy-start.5
  125.9 59.3 %all_to_all.11.in_ref = f32[256,16,128]{2,1,0:T(8,128)S(1)} all-to-all(f32[256,16,128]{2,1,0:T(8,128)S(1)} %bitcast.6), channel_id=1, replica_groups=mesh['x'=4,'y'=4,'zl'=2,'core'=2,'zh'=4] {'x','y','zh','zl','core'}, dimensions={0} | all-to-all | bytes 4194304 | tf_op jit(solution)/shard_map/all_to_all | solution.py:323
  185.1 0.0 copy-done.4
  185.1 0.0 copy-done.5
  185.1 2.3 %radial_back.1 = f32[8,2,256,128]{3,2,1,0:T(8,128)} custom-call(f32[256,16,128]{2,1,0:T(8,128)S(1)} %all_to_all.11.in_ref, bf16[256,256]{1,0:T(8,128)(2,1)S(1)} %copy-done.5, bf16[256,256]{1,0:T(8,128)(2,1)S(1)} %copy-done.4), custom_call_target="tpu_custom_call" | custom-call | tf_op jit(solution)/shard_map/radial_back/pallas_call | solution.py:311
Async XLA Ops:
  4.1 115.2 %copy-start = (bf16[4,2,256,256]{3,2,1,0:T(8,128)(2,1)S(1)}, bf16[4,2,256,256]{3,2,1,0:T(8,128)(2,1)}, u32[]{:S(2)}) copy-start(bf16[4,2,256,256]{3,2,1,0:T(8,128)(2,1)} %constant.21.clone.back_table_ref) | copy-start | bytes 3145732
  4.2 115.2 %copy-start.1 = (bf16[4,2,256,256]{3,2,1,0:T(8,128)(2,1)S(1)}, bf16[4,2,256,256]{3,2,1,0:T(8,128)(2,1)}, u32[]{:S(2)}) copy-start(bf16[4,2,256,256]{3,2,1,0:T(8,128)(2,1)} %constant.20.clone.out_table_ref) | copy-start | bytes 3145732
  4.2 115.2 %copy-start.2 = (bf16[2,2,256,256]{3,2,1,0:T(8,128)(2,1)S(1)}, bf16[2,2,256,256]{3,2,1,0:T(8,128)(2,1)}, u32[]{:S(2)}) copy-start(bf16[2,2,256,256]{3,2,1,0:T(8,128)(2,1)} %constant.19.clone.line_back_ref) | copy-start | bytes 1572868
  4.2 115.2 %copy-start.3 = (bf16[2,2,256,256]{3,2,1,0:T(8,128)(2,1)S(1)}, bf16[2,2,256,256]{3,2,1,0:T(8,128)(2,1)}, u32[]{:S(2)}) copy-start(bf16[2,2,256,256]{3,2,1,0:T(8,128)(2,1)} %constant.18.clone.line_out_ref) | copy-start | bytes 1572868
  125.8 59.3 %copy-start.4 = (bf16[256,256]{1,0:T(8,128)(2,1)S(1)}, bf16[256,256]{1,0:T(8,128)(2,1)}, u32[]{:S(2)}) copy-start(bf16[256,256]{1,0:T(8,128)(2,1)} %constant.23.clone.tl_ref) | copy-start | bytes 393220
  125.8 59.3 %copy-start.5 = (bf16[256,256]{1,0:T(8,128)(2,1)S(1)}, bf16[256,256]{1,0:T(8,128)(2,1)}, u32[]{:S(2)}) copy-start(bf16[256,256]{1,0:T(8,128)(2,1)} %constant.22.clone.th_ref) | copy-start | bytes 393220

commit v9 on v8

--- a/solution.py
+++ b/solution.py
@@ -74,23 +74,31 @@
         copy.wait()
     table = table_ref[0], table_ref[1]
 
-    def turn(field, first, last):
-        for group in (2 * field, 2 * field + 1):
-            rows = slice(8 * group, 8 * (group + 1))
-            out_ref[first:last, rows, :] = turn_ref[group, first:last]
-
-    for field in range(2):
-        for i in range(8):
-            if (field, i) in loads:
-                loads[field, i].wait()
-            pair = jnp.concatenate([x_ref[field, i, 0], x_ref[field, i, 1]], axis=1)
-            result = product(table, split(pair))
-            for parity in range(2):
-                rows = turn_ref.at[2 * field + parity].reshape(NR * 8, 128)
-                rows[pl.ds(i, NR, stride=8), :] = result[:, 128 * parity : 128 * (parity + 1)]
-            if field == 1:
-                turn(0, 32 * i, 32 * (i + 1))
-    turn(1, 0, NR)
+    def turn(group, first, last):
+        out_ref[first:last, 8 * group : 8 * (group + 1), :] = turn_ref[group, first:last]
+
+    def synthesize(field, places):
+        pair = jnp.concatenate([x_ref[field, i, parity] for i, parity in places], axis=1)
+        result = product(table, split(pair))
+        for k, (i, parity) in enumerate(places):
+            rows = turn_ref.at[2 * field + parity].reshape(NR * 8, 128)
+            rows[pl.ds(i, NR, stride=8), :] = result[:, 128 * k : 128 * (k + 1)]
+
+    for i in range(8):
+        if (0, i) in loads:
+            loads[0, i].wait()
+        synthesize(0, ((i, 0), (i, 1)))
+    loads[1, 0].wait()
+    for parity in range(2):
+        for i in range(0, 8, 2):
+            synthesize(1, ((i, parity), (i + 1, parity)))
+            first = 32 * i
+            if parity == 0:
+                turn(0, first, first + 64)
+                turn(1, first, first + 64)
+            else:
+                turn(2, first, first + 64)
+    turn(3, 0, NR)
 
 
 def radial_back(in_ref, th_ref, tl_ref, out_hbm, out_ref, sems):

time: 188 us -> 188 us (level)
  no operation moved by 1% of the time
where the time goes in v9:
time: 188 us
  blocking collectives  174 us (93%)
  Pallas kernels  13 us (7%)
    all_to_all x2, blocking collectives, exchange(): return lax.all_to_all(x, ORDER, split_axis=0, concat_axis=0, tiled=True)  174 us
    pallas_call x1, Pallas kernels, run_grid(): pl.pallas_call(grid_kernel, in_specs=[NEAR] * 5, out_specs=NEAR, out_shap...  6.42 us
    pallas_call x1, Pallas kernels, run_radial_out(): pl.pallas_call(radial_out, in_specs=[FAR] * 4, out_specs=NEAR, out_shape=...  4.21 us

profile of v9, /device:TPU:1, one launch (start us, length us, event | category | flops | bytes accessed | tf_op | source)
XLA Modules:
  0.0 187.5 jit_solution(17092904184892592240)
XLA Ops:
  0.0 4.2 %radial_out.1 = f32[256,32,128]{2,1,0:T(8,128)S(1)} custom-call(f32[8,2,256,128]{3,2,1,0:T(8,128)} %bitcast.7, f32[8,2,256,128]{3,2,1,0:T(8,128)} %bitcast.8, bf16[256,256]{1,0:T(8,128)(2,1)} %constant.16.clone.th_hbm, bf16[256,256]{1,0:T(8,128)(2,1)} %constant.17.clone.tl_hbm), custom_call_target="tpu_custom_call" | custom-call | tf_op jit(solution)/shard_map/radial_out/pallas_call | solution.py:279
  4.2 0.0 copy-start
  4.2 0.0 copy-start.1
  4.2 0.0 copy-start.2
  4.3 0.0 copy-start.3
  4.3 115.2 %all_to_all.10 = f32[256,32,128]{2,1,0:T(8,128)S(1)} all-to-all(f32[256,32,128]{2,1,0:T(8,128)S(1)} %radial_out.1), channel_id=1, replica_groups=mesh['x'=4,'y'=4,'zl'=2,'core'=2,'zh'=4] {'x','y','zh','zl','core'}, dimensions={0} | all-to-all | bytes 8388608 | tf_op jit(solution)/shard_map/all_to_all | solution.py:331
  119.5 0.0 copy-done
  119.5 0.0 copy-done.1
  119.5 0.0 copy-done.2
  119.5 0.0 copy-done.3
  119.5 6.4 %grid.1 = f32[16,4,4,2,8,128]{5,4,3,2,1,0:T(8,128)S(1)} custom-call(f32[16,4,4,2,2,8,128]{6,5,4,3,2,1,0:T(8,128)S(1)} %bitcast.5, bf16[2,2,256,256]{3,2,1,0:T(8,128)(2,1)S(1)} %copy-done.3, bf16[2,2,256,256]{3,2,1,0:T(8,128)(2,1)S(1)} %copy-done.2, bf16[4,2,256,256]{3,2,1,0:T(8,128)(2,1)S(1)} %copy-done.1, bf16[4,2,256,256]{3,2,1,0:T(8,128)(2,1)S(1)} %copy-done), custom_call_target="tpu_custom_call" | custom-call | tf_op jit(solution)/shard_map/grid/pallas_call | solution.py:300
  125.9 0.0 copy-start.4
  125.9 0.0 copy-start.5
  125.9 59.3 %all_to_all.11.in_ref = f32[256,16,128]{2,1,0:T(8,128)S(1)} all-to-all(f32[256,16,128]{2,1,0:T(8,128)S(1)} %bitcast.6), channel_id=1, replica_groups=mesh['x'=4,'y'=4,'zl'=2,'core'=2,'zh'=4] {'x','y','zh','zl','core'}, dimensions={0} | all-to-all | bytes 4194304 | tf_op jit(solution)/shard_map/all_to_all | solution.py:331
  185.2 0.0 copy-done.4
  185.2 0.0 copy-done.5
  185.2 2.3 %radial_back.1 = f32[8,2,256,128]{3,2,1,0:T(8,128)} custom-call(f32[256,16,128]{2,1,0:T(8,128)S(1)} %all_to_all.11.in_ref, bf16[256,256]{1,0:T(8,128)(2,1)S(1)} %copy-done.5, bf16[256,256]{1,0:T(8,128)(2,1)S(1)} %copy-done.4), custom_call_target="tpu_custom_call" | custom-call | tf_op jit(solution)/shard_map/radial_back/pallas_call | solution.py:319
Async XLA Ops:
  4.2 115.2 %copy-start = (bf16[4,2,256,256]{3,2,1,0:T(8,128)(2,1)S(1)}, bf16[4,2,256,256]{3,2,1,0:T(8,128)(2,1)}, u32[]{:S(2)}) copy-start(bf16[4,2,256,256]{3,2,1,0:T(8,128)(2,1)} %constant.21.clone.back_table_ref) | copy-start | bytes 3145732
  4.2 115.2 %copy-start.1 = (bf16[4,2,256,256]{3,2,1,0:T(8,128)(2,1)S(1)}, bf16[4,2,256,256]{3,2,1,0:T(8,128)(2,1)}, u32[]{:S(2)}) copy-start(bf16[4,2,256,256]{3,2,1,0:T(8,128)(2,1)} %constant.20.clone.out_table_ref) | copy-start | bytes 3145732
  4.2 115.2 %copy-start.2 = (bf16[2,2,256,256]{3,2,1,0:T(8,128)(2,1)S(1)}, bf16[2,2,256,256]{3,2,1,0:T(8,128)(2,1)}, u32[]{:S(2)}) copy-start(bf16[2,2,256,256]{3,2,1,0:T(8,128)(2,1)} %constant.19.clone.line_back_ref) | copy-start | bytes 1572868
  4.3 115.2 %copy-start.3 = (bf16[2,2,256,256]{3,2,1,0:T(8,128)(2,1)S(1)}, bf16[2,2,256,256]{3,2,1,0:T(8,128)(2,1)}, u32[]{:S(2)}) copy-start(bf16[2,2,256,256]{3,2,1,0:T(8,128)(2,1)} %constant.18.clone.line_out_ref) | copy-start | bytes 1572868
  125.9 59.3 %copy-start.4 = (bf16[256,256]{1,0:T(8,128)(2,1)S(1)}, bf16[256,256]{1,0:T(8,128)(2,1)}, u32[]{:S(2)}) copy-start(bf16[256,256]{1,0:T(8,128)(2,1)} %constant.23.clone.tl_ref) | copy-start | bytes 393220
  125.9 59.3 %copy-start.5 = (bf16[256,256]{1,0:T(8,128)(2,1)S(1)}, bf16[256,256]{1,0:T(8,128)(2,1)}, u32[]{:S(2)}) copy-start(bf16[256,256]{1,0:T(8,128)(2,1)} %constant.22.clone.th_ref) | copy-start | bytes 393220
